TPU v7x, 32 devices: a whole 2x2x4 slice. The times are simulated.
32 devices in a mesh: dp: 16 (over z, y, core), tensor: 2 (over x).
Axes of the slice: x: 2, y: 2, z: 4, core: 2. Of those that a mesh axis runs over, the one named last changes fastest.
Arguments:
- latents: bfloat16 [16384, 1024], P(('dp', 'tensor')), may hold values from -6 to 6
- inputs: bfloat16 [65536, 1024], P(('dp', 'tensor')), may hold values from -6 to 6
- frames: int32 [128], replicated, may hold values from 4 to 16, as said below
- group_clip: int32 [128], P('dp'), may hold values from 0 to 127, each once
- norm_gain: float32 [4, 1024], replicated, may hold values from 0.5 to 1.5
- norm_bias: float32 [4, 1024], replicated, may hold values from -2 to 2
- cross_q: bfloat16 [1024, 1024], P(None, 'tensor'), may hold values from -0.1875 to 0.1875
- cross_k: bfloat16 [1024, 1024], P(None, 'tensor'), may hold values from -0.1875 to 0.1875
- cross_v: bfloat16 [1024, 1024], P(None, 'tensor'), may hold values from -0.1875 to 0.1875
- cross_o: bfloat16 [1024, 1024], P('tensor'), may hold values from -1 to 1
- self_q: bfloat16 [1024, 1024], P(None, 'tensor'), may hold values from -0.1875 to 0.1875
- self_k: bfloat16 [1024, 1024], P(None, 'tensor'), may hold values from -0.1875 to 0.1875
- self_v: bfloat16 [1024, 1024], P(None, 'tensor'), may hold values from -0.1875 to 0.1875
- self_o: bfloat16 [1024, 1024], P('tensor'), may hold values from -0.75 to 0.75
- mlp_up: bfloat16 [1024, 4096], P(None, 'tensor'), may hold values from -0.1875 to 0.1875
- up_bias: bfloat16 [4096], P('tensor'), may hold values from -3 to 3
- mlp_down: bfloat16 [4096, 1024], P('tensor'), may hold values from -0.09375 to 0.09375
- out_bias: float32 [3, 1024], replicated, may hold values from -2 to 2
- cotangent: bfloat16 [16384, 1024], P(('dp', 'tensor')), may hold values from -6 to 6
Outputs:
- result: bfloat16 [16384, 1024], P(('dp', 'tensor'))
- d_latents: float32 [16384, 1024], P(('dp', 'tensor'))
- d_inputs: float32 [65536, 1024], P(('dp', 'tensor'))
- d_norm_gain: float32 [4, 1024], replicated
- d_norm_bias: float32 [4, 1024], replicated
- d_out_bias: float32 [3, 1024], replicated
- d_cross_q: float32 [1024, 1024], P(None, 'tensor')
- d_cross_k: float32 [1024, 1024], P(None, 'tensor')
- d_cross_v: float32 [1024, 1024], P(None, 'tensor')
- d_cross_o: float32 [1024, 1024], P('tensor')
- d_self_q: float32 [1024, 1024], P(None, 'tensor')
- d_self_k: float32 [1024, 1024], P(None, 'tensor')
- d_self_v: float32 [1024, 1024], P(None, 'tensor')
- d_self_o: float32 [1024, 1024], P('tensor')
- d_mlp_up: float32 [1024, 4096], P(None, 'tensor')
- d_up_bias: float32 [4096], P('tensor')
- d_mlp_down: float32 [4096, 1024], P('tensor')
Inputs may be any that keep to these rules, and one draw needn't show every extreme that they name: Each clip has 4 or 16 frames, and both counts occur. `group_clip`: every clip index belongs to exactly one group.
All inputs are finite; a program needn't handle non-finite values.
Results may differ from a plain program's by a relative error of at most 0.03.
Values may be sent and summed in bfloat16 or wider, within the bound.
A program may use at most 256 MiB of HBM per device.

v0:
```python
import jax
import jax.numpy as jnp
from jax import lax
from jax.sharding import PartitionSpec as P

HS = 128
LAT = 128
FRAME_ROWS = 32


EPSILON = 1e-05
NEG_LARGE = -1e30
GELU_COEF = 0.7978845608028654
GELU_CUBE = 0.044715


def layer_norm(values, gain, shift):
    average = jnp.mean(values, axis=-1, keepdims=True)
    centered = values - average
    variance = jnp.mean(centered * centered, axis=-1, keepdims=True)
    return centered * lax.rsqrt(variance + EPSILON) * gain + shift


def gelu_tanh(values):
    inner = GELU_COEF * (values + GELU_CUBE * values * values * values)
    return 0.5 * values * (1.0 + jnp.tanh(inner))


def gelu_slope(values):
    squared = values * values
    hyperbolic = jnp.tanh(GELU_COEF * (values + GELU_CUBE * squared * values))
    return 0.5 * (1.0 + hyperbolic) + 0.5 * values * (1.0 - hyperbolic * hyperbolic) * GELU_COEF * (
        1.0 + 3.0 * GELU_CUBE * squared
    )


def matmul(left, right):
    return jnp.dot(left, right, preferred_element_type=jnp.float32)


def gram_left(left, right):
    return lax.dot_general(
        left, right, (((0,), (0,)), ((), ())), preferred_element_type=jnp.float32
    )


def times_transposed(left, right):
    return lax.dot_general(
        left, right, (((1,), (1,)), ((), ())), preferred_element_type=jnp.float32
    )


def block_size(groups):
    chosen = 1
    for candidate in (4, 3, 2):
        if chosen == 1 and groups % candidate == 0:
            chosen = candidate
    return chosen


def split_blocks(array, groups, head_size):
    block = block_size(groups)
    rows = array.shape[0] // groups
    heads = array.shape[1] // head_size
    return array.reshape(groups // block, block, rows, heads, head_size)


def masked_scores(query_block, key_block, length_block, head_size):
    key_count = key_block.shape[1]
    scores = jnp.einsum(
        "gqhd,gkhd->ghqk", query_block, key_block, preferred_element_type=jnp.float32
    ) * head_size ** (-0.5)
    positions = lax.broadcasted_iota(jnp.int32, (1, 1, 1, key_count), 3)
    return jnp.where(positions < length_block[:, None, None, None], scores, NEG_LARGE)


def attend_forward(queries, key_vecs, value_vecs, lengths, head_size):
    groups = lengths.shape[0]
    block = block_size(groups)
    pieces = (
        split_blocks(queries, groups, head_size),
        split_blocks(key_vecs, groups, head_size),
        split_blocks(value_vecs, groups, head_size),
        lengths.reshape(groups // block, block),
    )

    def one_block(piece):
        query_block, key_block, value_block, length_block = piece
        scores = masked_scores(query_block, key_block, length_block, head_size)
        row_max = jnp.max(scores, axis=-1, keepdims=True)
        exponent = jnp.exp(scores - row_max)
        row_total = jnp.sum(exponent, axis=-1, keepdims=True)
        probability = (exponent / row_total).astype(jnp.bfloat16)
        mixed = jnp.einsum(
            "ghqk,gkhd->gqhd", probability, value_block, preferred_element_type=jnp.float32
        )
        return (mixed.astype(jnp.bfloat16), (row_max + jnp.log(row_total))[..., 0])

    mixed, log_total = lax.map(one_block, pieces)
    return (mixed.reshape(queries.shape), log_total)


def attend_backward(queries, key_vecs, value_vecs, grad_mixed, log_total, lengths, head_size):
    groups = lengths.shape[0]
    block = block_size(groups)
    pieces = (
        split_blocks(queries, groups, head_size),
        split_blocks(key_vecs, groups, head_size),
        split_blocks(value_vecs, groups, head_size),
        split_blocks(grad_mixed, groups, head_size),
        log_total,
        lengths.reshape(groups // block, block),
    )
    scale_factor = head_size ** (-0.5)

    def one_block(piece):
        query_block, key_block, value_block, grad_block, total_block, length_block = piece
        scores = masked_scores(query_block, key_block, length_block, head_size)
        probability = jnp.exp(scores - total_block[..., None])
        grad_prob = jnp.einsum(
            "gqhd,gkhd->ghqk", grad_block, value_block, preferred_element_type=jnp.float32
        )
        inner = jnp.sum(probability * grad_prob, axis=-1, keepdims=True)
        grad_score = (probability * (grad_prob - inner)).astype(jnp.bfloat16)
        grad_query = (
            jnp.einsum("ghqk,gkhd->gqhd", grad_score, key_block, preferred_element_type=jnp.float32)
            * scale_factor
        )
        grad_key = (
            jnp.einsum(
                "ghqk,gqhd->gkhd", grad_score, query_block, preferred_element_type=jnp.float32
            )
            * scale_factor
        )
        grad_value = jnp.einsum(
            "ghqk,gqhd->gkhd",
            probability.astype(jnp.bfloat16),
            grad_block,
            preferred_element_type=jnp.float32,
        )
        return (
            grad_query.astype(jnp.bfloat16),
            grad_key.astype(jnp.bfloat16),
            grad_value.astype(jnp.bfloat16),
        )

    grad_query, grad_key, grad_value = lax.map(one_block, pieces)
    return (
        grad_query.reshape(queries.shape),
        grad_key.reshape(key_vecs.shape),
        grad_value.reshape(value_vecs.shape),
    )


def gather_rows(normed):
    return lax.all_gather(normed, "tensor", axis=0, tiled=True)


def gather_grads(grads):
    return lax.all_gather(grads, "tensor", axis=0, tiled=True)


def branch_sum(mixed, weight, own_rows):

    def term(begin_row, row_count):
        return matmul(mixed, weight)

    return lax.psum_scatter(
        term(jnp.int32(0), lax.axis_size("tensor") * own_rows),
        "tensor",
        scatter_dimension=0,
        tiled=True,
    )


def back_rows(term, own_rows):
    return lax.psum_scatter(
        term(jnp.int32(0), own_rows * lax.axis_size("tensor")).astype(jnp.bfloat16),
        "tensor",
        scatter_dimension=0,
        tiled=True,
    ).astype(jnp.float32)


def back_inputs(term, own_rows):
    return lax.psum_scatter(
        term(jnp.int32(0), own_rows * lax.axis_size("tensor")).astype(jnp.bfloat16),
        "tensor",
        scatter_dimension=0,
        tiled=True,
    ).astype(jnp.float32)


def shards(
    latents,
    inputs,
    frames,
    group_clip,
    norm_gain,
    norm_bias,
    cross_q,
    cross_k,
    cross_v,
    cross_o,
    self_q,
    self_k,
    self_v,
    self_o,
    mlp_up,
    up_bias,
    mlp_down,
    out_bias,
    cotangent,
):
    head_size = HS
    own_rows = latents.shape[0]
    own_inputs = inputs.shape[0]
    stream = latents.astype(jnp.float32)
    source = inputs.astype(jnp.float32)
    lat_normed = layer_norm(stream, norm_gain[0], norm_bias[0]).astype(jnp.bfloat16)
    in_normed = layer_norm(source, norm_gain[1], norm_bias[1]).astype(jnp.bfloat16)
    local_set = (
        cross_q,
        cross_k,
        cross_v,
        cross_o,
        self_q,
        self_k,
        self_v,
        self_o,
        mlp_up,
        up_bias,
        mlp_down,
    )
    rows_cross, rows_input = (
        lax.all_gather(lat_normed, "tensor", axis=0, tiled=True),
        lax.all_gather(in_normed, "tensor", axis=0, tiled=True),
    )
    (
        w_cross_q,
        w_cross_k,
        w_cross_v,
        w_cross_o,
        w_self_q,
        w_self_k,
        w_self_v,
        w_self_o,
        w_up,
        b_up,
        w_down,
    ) = local_set
    matches = group_clip[:, None] == lax.broadcasted_iota(jnp.int32, (1, frames.shape[0]), 1)
    lengths = jnp.sum(jnp.where(matches, frames[None, :], 0), axis=1) * FRAME_ROWS
    full_lengths = jnp.full(lengths.shape, LAT, jnp.int32)
    cross_query = matmul(rows_cross, w_cross_q).astype(jnp.bfloat16)
    cross_keys = matmul(rows_input, w_cross_k).astype(jnp.bfloat16)
    cross_values = matmul(rows_input, w_cross_v).astype(jnp.bfloat16)
    cross_mixed, cross_total = attend_forward(
        cross_query, cross_keys, cross_values, lengths, head_size
    )
    stream1 = stream + branch_sum(cross_mixed, w_cross_o, own_rows) + out_bias[0]
    self_normed = layer_norm(stream1, norm_gain[2], norm_bias[2]).astype(jnp.bfloat16)
    rows_self = gather_rows(self_normed)
    self_query = matmul(rows_self, w_self_q).astype(jnp.bfloat16)
    self_keys = matmul(rows_self, w_self_k).astype(jnp.bfloat16)
    self_values = matmul(rows_self, w_self_v).astype(jnp.bfloat16)
    self_mixed, self_total = attend_forward(
        self_query, self_keys, self_values, full_lengths, head_size
    )
    stream2 = stream1 + branch_sum(self_mixed, w_self_o, own_rows) + out_bias[1]
    mlp_normed = layer_norm(stream2, norm_gain[3], norm_bias[3]).astype(jnp.bfloat16)
    rows_mlp = gather_rows(mlp_normed)
    pre_act = matmul(rows_mlp, w_up) + b_up.astype(jnp.float32)
    hidden = gelu_tanh(pre_act).astype(jnp.bfloat16)
    stream3 = stream2 + branch_sum(hidden, w_down, own_rows) + out_bias[2]
    result = stream3.astype(jnp.bfloat16)
    grad3 = cotangent.astype(jnp.float32)
    rows_grad3 = gather_grads(grad3.astype(jnp.bfloat16))
    d_down = gram_left(hidden, rows_grad3)
    d_pre = (times_transposed(rows_grad3, w_down) * gelu_slope(pre_act)).astype(jnp.bfloat16)
    d_upb = jnp.sum(d_pre.astype(jnp.float32), axis=0)
    d_up = gram_left(rows_mlp, d_pre)
    d_mlp_rows = back_rows(lambda begin_row, row_count: times_transposed(d_pre, w_up), own_rows)
    ln_value, ln_pull = jax.vjp(layer_norm, stream2, norm_gain[3], norm_bias[3])
    d_stream2, gain_three, shift_three = ln_pull(d_mlp_rows)
    grad2 = grad3 + d_stream2
    rows_grad2 = gather_grads(grad2.astype(jnp.bfloat16))
    self_query = matmul(rows_self, w_self_q).astype(jnp.bfloat16)
    self_keys = matmul(rows_self, w_self_k).astype(jnp.bfloat16)
    self_values = matmul(rows_self, w_self_v).astype(jnp.bfloat16)
    self_mixed, self_total = attend_forward(
        self_query, self_keys, self_values, full_lengths, head_size
    )
    d_self_o = gram_left(self_mixed, rows_grad2)
    d_self_mixed = times_transposed(rows_grad2, w_self_o).astype(jnp.bfloat16)
    d_self_query, d_self_keys, d_self_values = attend_backward(
        self_query, self_keys, self_values, d_self_mixed, self_total, full_lengths, head_size
    )
    d_self_q = gram_left(rows_self, d_self_query)
    d_self_k = gram_left(rows_self, d_self_keys)
    d_self_v = gram_left(rows_self, d_self_values)

    def self_term(begin_row, row_count):
        return (
            times_transposed(d_self_query, w_self_q)
            + times_transposed(d_self_keys, w_self_k)
            + times_transposed(d_self_values, w_self_v)
        )

    d_self_rows = back_rows(self_term, own_rows)
    ln_value, ln_pull = jax.vjp(layer_norm, stream1, norm_gain[2], norm_bias[2])
    d_stream1, gain_two, shift_two = ln_pull(d_self_rows)
    grad1 = grad2 + d_stream1
    rows_grad1 = gather_grads(grad1.astype(jnp.bfloat16))
    d_cross_o = gram_left(cross_mixed, rows_grad1)
    d_cross_mixed = times_transposed(rows_grad1, w_cross_o).astype(jnp.bfloat16)
    d_cross_query, d_cross_keys, d_cross_values = attend_backward(
        cross_query, cross_keys, cross_values, d_cross_mixed, cross_total, lengths, head_size
    )
    d_cross_q = gram_left(rows_cross, d_cross_query)
    d_cross_k = gram_left(rows_input, d_cross_keys)
    d_cross_v = gram_left(rows_input, d_cross_values)
    d_lat_rows = back_rows(
        lambda begin_row, row_count: times_transposed(d_cross_query, w_cross_q), own_rows
    )

    def input_term(begin_row, row_count):
        return times_transposed(d_cross_keys, w_cross_k) + times_transposed(
            d_cross_values, w_cross_v
        )

    d_in_rows = back_inputs(input_term, own_inputs)
    ln_value, ln_pull = jax.vjp(layer_norm, stream, norm_gain[0], norm_bias[0])
    d_stream0, gain_zero, shift_zero = ln_pull(d_lat_rows)
    d_latents = grad1 + d_stream0
    ln_value, ln_pull = jax.vjp(layer_norm, source, norm_gain[1], norm_bias[1])
    d_inputs, gain_one, shift_one = ln_pull(d_in_rows)
    gain_grads = jnp.stack([gain_zero, gain_one, gain_two, gain_three])
    shift_grads = jnp.stack([shift_zero, shift_one, shift_two, shift_three])
    bias_grads = jnp.stack([jnp.sum(grad1, axis=0), jnp.sum(grad2, axis=0), jnp.sum(grad3, axis=0)])
    gain_grads, shift_grads, bias_grads = lax.psum(
        (gain_grads, shift_grads, bias_grads), ("dp", "tensor")
    )
    (
        d_cross_q,
        d_cross_k,
        d_cross_v,
        d_cross_o,
        d_self_q,
        d_self_k,
        d_self_v,
        d_self_o,
        d_up,
        d_upb,
        d_down,
    ) = (
        lax.psum(d_cross_q.astype(jnp.bfloat16), "dp").astype(jnp.float32),
        lax.psum(d_cross_k.astype(jnp.bfloat16), "dp").astype(jnp.float32),
        lax.psum(d_cross_v.astype(jnp.bfloat16), "dp").astype(jnp.float32),
        lax.psum(d_cross_o.astype(jnp.bfloat16), "dp").astype(jnp.float32),
        lax.psum(d_self_q.astype(jnp.bfloat16), "dp").astype(jnp.float32),
        lax.psum(d_self_k.astype(jnp.bfloat16), "dp").astype(jnp.float32),
        lax.psum(d_self_v.astype(jnp.bfloat16), "dp").astype(jnp.float32),
        lax.psum(d_self_o.astype(jnp.bfloat16), "dp").astype(jnp.float32),
        lax.psum(d_up.astype(jnp.bfloat16), "dp").astype(jnp.float32),
        lax.psum(d_upb.astype(jnp.bfloat16), "dp").astype(jnp.float32),
        lax.psum(d_down.astype(jnp.bfloat16), "dp").astype(jnp.float32),
    )
    return (
        result,
        d_latents,
        d_inputs,
        gain_grads,
        shift_grads,
        bias_grads,
        d_cross_q,
        d_cross_k,
        d_cross_v,
        d_cross_o,
        d_self_q,
        d_self_k,
        d_self_v,
        d_self_o,
        d_up,
        d_upb,
        d_down,
    )


def solution(mesh):
    in_specs = (
        P(("dp", "tensor"), None),
        P(("dp", "tensor"), None),
        P(),
        P("dp"),
        P(),
        P(),
        P(None, "tensor"),
        P(None, "tensor"),
        P(None, "tensor"),
        P("tensor", None),
        P(None, "tensor"),
        P(None, "tensor"),
        P(None, "tensor"),
        P("tensor", None),
        P(None, "tensor"),
        P("tensor"),
        P("tensor", None),
        P(),
        P(("dp", "tensor"), None),
    )
    out_specs = (
        P(("dp", "tensor"), None),
        P(("dp", "tensor"), None),
        P(("dp", "tensor"), None),
        P(),
        P(),
        P(),
        P(None, "tensor"),
        P(None, "tensor"),
        P(None, "tensor"),
        P("tensor", None),
        P(None, "tensor"),
        P(None, "tensor"),
        P(None, "tensor"),
        P("tensor", None),
        P(None, "tensor"),
        P("tensor"),
        P("tensor", None),
    )
    return jax.shard_map(shards, mesh=mesh, in_specs=in_specs, out_specs=out_specs, check_vma=False)
```

profile of v0, /device:TPU:0, one launch (start us, length us, event | category | flops | bytes accessed | tf_op | source)
XLA Modules:
  0.0 1340.8 jit_solution(18422580686185604196)
XLA Ops:
  24.9 26.5 %all-gather.10.cloned.1.call-done = bf16[1024,1024]{1,0:T(8,128)(2,1)} async-done(((bf16[512,1024]{1,0:T(8,128)(2,1)}), bf16[1024,1024]{1,0:T(8,128)(2,1)}) %all-gather.10.cloned.1.call-update) | async-done | bytes 2097168 | tf_op jit(solution)/shard_map/all_gather | solution.py:236
  56.0 101.6 %all-gather.8.cloned.1.call-done = bf16[4096,1024]{1,0:T(8,128)(2,1)} async-done(((bf16[2048,1024]{1,0:T(8,128)(2,1)}), bf16[4096,1024]{1,0:T(8,128)(2,1)}) %all-gather.8.cloned.1.call-update) | async-done | bytes 8388624 | tf_op jit(solution)/shard_map/all_gather | solution.py:237
  196.8 24.9 %while.62 = (s32[]{:T(128)}, bf16[2,4,128,4,128]{4,3,2,1,0:T(4,128)(2,1)}, f32[2,4,4,128]{3,2,1,0:T(4,128)S(1)}, bf16[2,4,512,4,128]{4,3,2,1,0:T(4,128)(2,1)}, s...) while((s32[]{:T(128)}, ...), condition=%wide.region_8.9_spmd, body=%wide.region_5.8_spmd.sunk | while | flops 549715968 | bytes 45163760 | solution.py:99
  227.2 53.8 %reduce-scatter.8.cloned.1.call-done = f32[512,1024]{1,0:T(8,128)} async-done(((f32[1024,1024]{1,0:T(8,128)}), f32[512,1024]{1,0:T(8,128)}) %reduce-scatter.8.cloned.1.call-update) | async-done | bytes 2097168 | tf_op jit(solution)/shard_map/reduce_scatter | solution.py:168
  285.1 33.2 %all-gather.12.cloned.1.call-done = bf16[1024,1024]{1,0:T(8,128)(2,1)} async-done(((bf16[512,1024]{1,0:T(8,128)(2,1)}), bf16[1024,1024]{1,0:T(8,128)(2,1)}) %all-gather.12.cloned.1.call-update) | async-done | bytes 2097168 | tf_op jit(solution)/shard_map/all_gather | solution.py:156
  345.4 18.6 %while.63 = (s32[]{:T(128)}, bf16[2,4,128,4,128]{4,3,2,1,0:T(4,128)(2,1)}, bf16[2,4,128,4,128]{2,4,3,1,0:T(8,128)(2,1)}, bf16[2,4,128,4,128]{4,2,3,1,0:T(8,128)(...) while((s32[]{:T(128)}, bf16[2,4,128,4,128]{4,3,2,1,0:T(4,128)(2,1)}, ...), condition=%wide.region_15.16_spmd, body=%wide.region_12.15_spmd.sunk | while | flops 136053376 | bytes 6309973 | solution.py:99
  368.9 54.5 %reduce-scatter.10.cloned.1.call-done = f32[512,1024]{1,0:T(8,128)} async-done(((f32[1024,1024]{1,0:T(8,128)}), f32[512,1024]{1,0:T(8,128)}) %reduce-scatter.10.cloned.1.call-update) | async-done | bytes 2097168 | tf_op jit(solution)/shard_map/reduce_scatter | solution.py:168
  429.3 32.0 %all-gather.14.cloned.1.call-done = bf16[1024,1024]{1,0:T(8,128)(2,1)} async-done(((bf16[512,1024]{1,0:T(8,128)(2,1)}), bf16[1024,1024]{1,0:T(8,128)(2,1)}) %all-gather.14.cloned.1.call-update) | async-done | bytes 2097168 | tf_op jit(solution)/shard_map/all_gather | solution.py:156
  472.1 23.8 %all-gather.16.cloned.1.call-done = bf16[1024,1024]{1,0:T(8,128)(2,1)} async-done(((bf16[512,1024]{1,0:T(8,128)(2,1)}), bf16[1024,1024]{1,0:T(8,128)(2,1)}) %all-gather.16.cloned.1.call-update) | async-done | bytes 2097168 | tf_op jit(solution)/shard_map/all_gather | solution.py:160
  495.9 13.1 fusion.227
  517.0 11.8 fusion.211
  528.9 19.9 %reduce-scatter.14.cloned.1.call-done = bf16[512,1024]{1,0:T(8,128)(2,1)} async-done(((bf16[1024,1024]{1,0:T(8,128)(2,1)}), bf16[512,1024]{1,0:T(8,128)(2,1)}) %reduce-scatter.14.cloned.1.call-update) | async-done | bytes 1048592 | tf_op jit(solution)/shard_map/reduce_scatter | solution.py:177
  551.5 54.1 %reduce-scatter.12.cloned.1.call-done = f32[512,1024]{1,0:T(8,128)} async-done(((f32[1024,1024]{1,0:T(8,128)}), f32[512,1024]{1,0:T(8,128)}) %reduce-scatter.12.cloned.1.call-update) | async-done | bytes 2097168 | tf_op jit(solution)/shard_map/reduce_scatter | solution.py:168
  623.2 22.8 %all-gather.18.cloned.1.call-done = bf16[1024,1024]{1,0:T(8,128)(2,1)} async-done(((bf16[512,1024]{1,0:T(8,128)(2,1)}), bf16[1024,1024]{1,0:T(8,128)(2,1)}) %all-gather.18.cloned.1.call-update) | async-done | bytes 2097168 | tf_op jit(solution)/shard_map/all_gather | solution.py:160
  656.0 22.7 %while.65 = (s32[]{:T(128)}, bf16[2,4,128,4,128]{4,3,2,1,0:T(4,128)(2,1)}, bf16[2,4,128,4,128]{4,3,2,1,0:T(4,128)(2,1)}, bf16[2,4,128,4,128]{4,3,2,1,0:T(4,128)(...) while((s32[]{:T(128)}, ...), condition=%wide.region_29.30_spmd, body=%wide.region_27.29_spmd.sunk | while | flops 339212800 | bytes 40413460 | solution.py:147
  686.3 12.6 convolution_convert_fusion.5
  698.9 19.1 %reduce-scatter.16.cloned.1.call-done = bf16[512,1024]{1,0:T(8,128)(2,1)} async-done(((bf16[1024,1024]{1,0:T(8,128)(2,1)}), bf16[512,1024]{1,0:T(8,128)(2,1)}) %reduce-scatter.16.cloned.1.call-update) | async-done | bytes 1048592 | tf_op jit(solution)/shard_map/reduce_scatter | solution.py:177
  744.7 16.3 %all-gather.20.cloned.1.call-done = bf16[1024,1024]{1,0:T(8,128)(2,1)} async-done(((bf16[512,1024]{1,0:T(8,128)(2,1)}), bf16[1024,1024]{1,0:T(8,128)(2,1)}) %all-gather.20.cloned.1.call-update) | async-done | bytes 2097168 | tf_op jit(solution)/shard_map/all_gather | solution.py:160
  765.6 64.0 %while.66 = (s32[]{:T(128)}, bf16[2,4,128,4,128]{4,3,2,1,0:T(4,128)(2,1)}, bf16[2,4,512,4,128]{4,3,2,1,0:T(4,128)(2,1)}, bf16[2,4,512,4,128]{4,3,2,1,0:T(4,128)(...) while((s32[]{:T(128)}, ...), condition=%wide.region_35.36_spmd, body=%wide.region_33.35_spmd.sunk | while | flops 1361575936 | bytes 150537648 | solution.py:147
  868.0 11.4 add_convert_fusion
  880.0 35.8 %psum.110 = bf16[2048]{0:T(1024)(128)(2,1)S(1)} all-reduce(bf16[2048]{0:T(1024)(128)(2,1)S(1)} %copy-done.87), channel_id=1, replica_groups=mesh['dp'=16,'tensor'=2] {'dp'}, use_global_device_ids=true, to_apply=%region_66.67 | all-reduce | flops 2048 | bytes 8192 | tf_op jit(solution)/shard_map/psum | solution.py:366
  923.2 249.8 %all-reduce.4.cloned.1.call-done = (bf16[1024,512]{1,0:T(8,128)(2,1)}, bf16[1024,512]{1,0:T(8,128)(2,1)}, bf16[1024,512]{1,0:T(8,128)(2,1)}, bf16[512,1024]{1,0:...) async-done(((bf16[1024,512]{1,0:T(8,128)(2,1)}, ...) | async-done | bytes 16777232 | tf_op jit(solution)/shard_map/psum | solution.py:357
  1197.4 77.4 %reduce-scatter.20.cloned.1.call-done = bf16[2048,1024]{1,0:T(8,128)(2,1)} async-done(((bf16[4096,1024]{1,0:T(8,128)(2,1)}), bf16[2048,1024]{1,0:T(8,128)(2,1)}) %reduce-scatter.20.cloned.1.call-update) | async-done | bytes 4194320 | tf_op jit(solution)/shard_map/reduce_scatter | solution.py:186
  1286.3 40.3 %all-reduce = (f32[4,1024]{1,0:T(4,128)}, f32[4,1024]{1,0:T(4,128)}, f32[3,1024]{1,0:T(4,128)}) all-reduce(f32[4,1024]{1,0:T(4,128)S(1)} %get-tuple-element.481, f32[4,1024]{1,0:T(4,128)S(1)} %get-tuple-element.482, f32[3,1024]{1,0:T(4,128)S(1)} %pad_maximum_fusion.2), channel_id=1, replica_groups=mesh['dp'=16,'tensor'=2] {'dp','tensor'}, use_global_device_ids=true, to_apply=%region_46.47 | all-reduce | flops 11264 | bytes 90112 | tf_op jit(solution)/shard_map/psum | solution.py:341
  (488 shorter events, 424.1 us)
Async XLA Ops:
  7.2 150.5 %copy-start = (bf16[1024,512]{1,0:T(8,128)(2,1)S(1)}, bf16[1024,512]{1,0:T(8,128)(2,1)}, u32[]{:S(2)}) copy-start(bf16[1024,512]{1,0:T(8,128)(2,1)} %param.36) | copy-start | bytes 3145732
  7.2 44.3 %all-gather.10.cloned.1.call-start = ((), (), s32[]{:S(2)}) async-start(), calls=%async_computation.8 | async-start | bytes 3145728 | tf_op jit(solution)/shard_map/all_gather | solution.py:236
  11.9 271.8 %copy-start.60 = (f32[1,1024]{1,0:T(1,128)}, f32[1,1024]{1,0:T(1,128)S(1)}, u32[]{:S(2)}) copy-start(f32[1,1024]{1,0:T(1,128)S(1)} %get-tuple-element.474) | copy-start | bytes 12292
  15.5 142.1 %all-gather.8.cloned.1.call-start = ((), (), s32[]{:S(2)}) async-start(), calls=%async_computation.7 | async-start | bytes 12582912 | tf_op jit(solution)/shard_map/all_gather | solution.py:237
  24.0 257.0 %reduce-scatter.8.cloned.1.call-start = ((), (), s32[]{:S(2)}) async-start(), calls=%async_computation.9 | async-start | bytes 6291456 | tf_op jit(solution)/shard_map/reduce_scatter | solution.py:168
  226.5 91.8 %all-gather.12.cloned.1.call-start = ((), (), s32[]{:S(2)}) async-start(), calls=%async_computation.10 | async-start | bytes 3145728 | tf_op jit(solution)/shard_map/all_gather | solution.py:156
  283.3 140.1 %copy-start.8 = (f32[512,1024]{1,0:T(8,128)}, f32[512,1024]{1,0:T(8,128)S(1)}, u32[]{:S(2)}) copy-start(f32[512,1024]{1,0:T(8,128)S(1)} %get-tuple-element.451) | copy-start | bytes 6291460
  285.1 138.3 %reduce-scatter.10.cloned.1.call-start = ((), (), s32[]{:S(2)}) async-start(), calls=%async_computation.11 | async-start | bytes 6291456 | tf_op jit(solution)/shard_map/reduce_scatter | solution.py:168
  368.9 92.4 %all-gather.14.cloned.1.call-start = ((), (), s32[]{:S(2)}) async-start(), calls=%async_computation.12 | async-start | bytes 3145728 | tf_op jit(solution)/shard_map/all_gather | solution.py:156
  428.0 67.9 %all-gather.16.cloned.1.call-start = ((), (), s32[]{:S(2)}) async-start(), calls=%async_computation.14 | async-start | bytes 3145728 | tf_op jit(solution)/shard_map/all_gather | solution.py:160
  428.8 120.1 %reduce-scatter.14.cloned.1.call-start = ((), (), s32[]{:S(2)}) async-start(), calls=%async_computation.15 | async-start | bytes 3145728 | tf_op jit(solution)/shard_map/reduce_scatter | solution.py:177
  516.8 88.8 %reduce-scatter.12.cloned.1.call-start = ((), (), s32[]{:S(2)}) async-start(), calls=%async_computation.13 | async-start | bytes 6291456 | tf_op jit(solution)/shard_map/reduce_scatter | solution.py:168
  528.8 117.1 %all-gather.18.cloned.1.call-start = ((), (), s32[]{:S(2)}) async-start(), calls=%async_computation.16 | async-start | bytes 3145728 | tf_op jit(solution)/shard_map/all_gather | solution.py:160
  612.7 105.3 %reduce-scatter.16.cloned.1.call-start = ((), (), s32[]{:S(2)}) async-start(), calls=%async_computation.17 | async-start | bytes 3145728 | tf_op jit(solution)/shard_map/reduce_scatter | solution.py:177
  685.9 75.1 %all-gather.20.cloned.1.call-start = ((), (), s32[]{:S(2)}) async-start(), calls=%async_computation.18 | async-start | bytes 3145728 | tf_op jit(solution)/shard_map/all_gather | solution.py:160
  727.8 188.8 %reduce-scatter.18.cloned.1.call-start = ((), (), s32[]{:S(2)}) async-start(), calls=%async_computation.19 | async-start | bytes 3145728 | tf_op jit(solution)/shard_map/reduce_scatter | solution.py:177
  833.9 339.1 %all-reduce.4.cloned.1.call-start = ((), (), s32[]{:S(2)}) async-start(), calls=%async_computation.21 | async-start | bytes 33554432 | tf_op jit(solution)/shard_map/psum | solution.py:357
  857.4 417.4 %reduce-scatter.20.cloned.1.call-start = ((), (), s32[]{:S(2)}) async-start(), calls=%async_computation.20 | async-start | bytes 12582912 | tf_op jit(solution)/shard_map/reduce_scatter | solution.py:186
  879.4 39.2 %copy-start.75 = (f32[512]{0:T(512)S(1)}, f32[512]{0:T(512)}, u32[]{:S(2)}) copy-start(f32[512]{0:T(512)} %copy-done.74) | copy-start | bytes 6148
  879.4 39.3 %copy-start.73 = (f32[512]{0:T(512)S(1)}, f32[512]{0:T(512)}, u32[]{:S(2)}) copy-start(f32[512]{0:T(512)} %copy-done.72) | copy-start | bytes 6148
  1193.0 81.9 %copy-start.53 = (f32[2048]{0:T(1024)S(1)}, f32[2048]{0:T(1024)}, u32[]{:S(2)}) copy-start(f32[2048]{0:T(1024)} %copy-done.52) | copy-start | bytes 24580
  1193.0 81.9 %copy-start.59 = (f32[1,1024]{1,0:T(1,128)S(1)}, f32[1,1024]{1,0:T(1,128)}, u32[]{:S(2)}) copy-start(f32[1,1024]{1,0:T(1,128)} %copy-done.58) | copy-start | bytes 12292
  1197.4 83.3 %copy-start.65 = (f32[2048]{0:T(1024)S(1)}, f32[2048]{0:T(1024)}, u32[]{:S(2)}) copy-start(f32[2048]{0:T(1024)} %copy-done.64) | copy-start | bytes 24580
  1197.4 83.3 %copy-start.57 = (f32[2048]{0:T(1024)S(1)}, f32[2048]{0:T(1024)}, u32[]{:S(2)}) copy-start(f32[2048]{0:T(1024)} %copy-done.56) | copy-start | bytes 24580
  (112 other events, 1002.9 us)
Sparse Core Ops, SparseCore 0:
  15.6 35.8 all-gather.9
  53.6 104.0 all-gather.7
  226.7 54.3 reduce-scatter.7
  285.2 33.0 all-gather.11
  369.0 54.3 reduce-scatter.9
  428.1 33.0 all-gather.13
  462.8 33.0 all-gather.15
  516.9 31.8 reduce-scatter.13
  551.1 54.3 reduce-scatter.11
  612.8 33.0 all-gather.17
  686.0 31.8 reduce-scatter.15
  727.9 33.0 all-gather.19
  834.0 31.8 reduce-scatter.17
  873.9 298.9 all-reduce.3
  1175.7 99.0 reduce-scatter.19
where the time goes:
time: 1350 us; the launch traced here: 1340 us
  waiting for transfers between devices  786 us (58%)
  matrix products  230 us (17%)
  local copies, waits for them, and re-layouts  137 us (10%)
  other arithmetic  93.8 us (7%)
  blocking collectives  76.1 us (6%)
  between operations  15.2 us (1%)
    psum x1, waiting for transfers between devices, shards(): lax.psum(d_cross_q.astype(jnp.bfloat16), 'dp').astype(jnp.float32)  250 us
    reduce_scatter x3, waiting for transfers between devices, branch_sum(): lax.psum_scatter(term(jnp.int32(0), lax.axis_size('tensor') * own_rows),...  162 us
    all_gather x1, waiting for transfers between devices, shards(): lax.all_gather(in_normed, 'tensor', axis=0, tiled=True)  102 us
    reduce_scatter x1, waiting for transfers between devices, back_inputs(): lax.psum_scatter(term(jnp.int32(0), own_rows * lax.axis_size('tensor')).a...  77.4 us
    dot_general x10, matrix products, matmul(): return jnp.dot(left, right, preferred_element_type=jnp.float32)  66.2 us
    all_gather x2, waiting for transfers between devices, gather_rows(): return lax.all_gather(normed, 'tensor', axis=0, tiled=True)  65.2 us
    all_gather x3, waiting for transfers between devices, gather_grads(): return lax.all_gather(grads, 'tensor', axis=0, tiled=True)  62.9 us
    dot_general x10, matrix products, times_transposed(): lax.dot_general(left, right, (((1,), (1,)), ((), ())), preferred_element_...  58.8 us
  transfers between devices with their start and end apart: 15, of which 14 were waited for; matrix products, arithmetic and copies ran while one was open for 11% of the time, Pallas kernels for 0%

commit v1 on v0

--- a/solution.py
+++ b/solution.py
@@ -1,8 +1,13 @@
+from types import SimpleNamespace
+
 import jax
 import jax.numpy as jnp
 from jax import lax
+from jax.experimental import pallas as pl
+from jax.experimental.pallas import tpu as pltpu
 from jax.sharding import PartitionSpec as P
 
+AXES = ("dp", "tensor")
 HS = 128
 LAT = 128
 FRAME_ROWS = 32
@@ -153,11 +158,11 @@
 
 
 def gather_rows(normed):
-    return lax.all_gather(normed, "tensor", axis=0, tiled=True)
+    return lax.all_gather(normed, AXES[1], axis=0, tiled=True)
 
 
 def gather_grads(grads):
-    return lax.all_gather(grads, "tensor", axis=0, tiled=True)
+    return lax.all_gather(grads, AXES[1], axis=0, tiled=True)
 
 
 def branch_sum(mixed, weight, own_rows):
@@ -166,8 +171,8 @@
         return matmul(mixed, weight)
 
     return lax.psum_scatter(
-        term(jnp.int32(0), lax.axis_size("tensor") * own_rows),
-        "tensor",
+        term(jnp.int32(0), lax.axis_size(AXES[1]) * own_rows),
+        AXES[1],
         scatter_dimension=0,
         tiled=True,
     )
@@ -175,8 +180,8 @@
 
 def back_rows(term, own_rows):
     return lax.psum_scatter(
-        term(jnp.int32(0), own_rows * lax.axis_size("tensor")).astype(jnp.bfloat16),
-        "tensor",
+        term(jnp.int32(0), own_rows * lax.axis_size(AXES[1])).astype(jnp.bfloat16),
+        AXES[1],
         scatter_dimension=0,
         tiled=True,
     ).astype(jnp.float32)
@@ -184,14 +189,14 @@
 
 def back_inputs(term, own_rows):
     return lax.psum_scatter(
-        term(jnp.int32(0), own_rows * lax.axis_size("tensor")).astype(jnp.bfloat16),
-        "tensor",
+        term(jnp.int32(0), own_rows * lax.axis_size(AXES[1])).astype(jnp.bfloat16),
+        AXES[1],
         scatter_dimension=0,
         tiled=True,
     ).astype(jnp.float32)
 
 
-def shards(
+def split_shards(
     latents,
     inputs,
     frames,
@@ -233,8 +238,8 @@
         mlp_down,
     )
     rows_cross, rows_input = (
-        lax.all_gather(lat_normed, "tensor", axis=0, tiled=True),
-        lax.all_gather(in_normed, "tensor", axis=0, tiled=True),
+        lax.all_gather(lat_normed, AXES[1], axis=0, tiled=True),
+        lax.all_gather(in_normed, AXES[1], axis=0, tiled=True),
     )
     (
         w_cross_q,
@@ -339,7 +344,7 @@
     shift_grads = jnp.stack([shift_zero, shift_one, shift_two, shift_three])
     bias_grads = jnp.stack([jnp.sum(grad1, axis=0), jnp.sum(grad2, axis=0), jnp.sum(grad3, axis=0)])
     gain_grads, shift_grads, bias_grads = lax.psum(
-        (gain_grads, shift_grads, bias_grads), ("dp", "tensor")
+        (gain_grads, shift_grads, bias_grads), AXES
     )
     (
         d_cross_q,
@@ -354,17 +359,17 @@
         d_upb,
         d_down,
     ) = (
-        lax.psum(d_cross_q.astype(jnp.bfloat16), "dp").astype(jnp.float32),
-        lax.psum(d_cross_k.astype(jnp.bfloat16), "dp").astype(jnp.float32),
-        lax.psum(d_cross_v.astype(jnp.bfloat16), "dp").astype(jnp.float32),
-        lax.psum(d_cross_o.astype(jnp.bfloat16), "dp").astype(jnp.float32),
-        lax.psum(d_self_q.astype(jnp.bfloat16), "dp").astype(jnp.float32),
-        lax.psum(d_self_k.astype(jnp.bfloat16), "dp").astype(jnp.float32),
-        lax.psum(d_self_v.astype(jnp.bfloat16), "dp").astype(jnp.float32),
-        lax.psum(d_self_o.astype(jnp.bfloat16), "dp").astype(jnp.float32),
-        lax.psum(d_up.astype(jnp.bfloat16), "dp").astype(jnp.float32),
-        lax.psum(d_upb.astype(jnp.bfloat16), "dp").astype(jnp.float32),
-        lax.psum(d_down.astype(jnp.bfloat16), "dp").astype(jnp.float32),
+        lax.psum(d_cross_q.astype(jnp.bfloat16), AXES[0]).astype(jnp.float32),
+        lax.psum(d_cross_k.astype(jnp.bfloat16), AXES[0]).astype(jnp.float32),
+        lax.psum(d_cross_v.astype(jnp.bfloat16), AXES[0]).astype(jnp.float32),
+        lax.psum(d_cross_o.astype(jnp.bfloat16), AXES[0]).astype(jnp.float32),
+        lax.psum(d_self_q.astype(jnp.bfloat16), AXES[0]).astype(jnp.float32),
+        lax.psum(d_self_k.astype(jnp.bfloat16), AXES[0]).astype(jnp.float32),
+        lax.psum(d_self_v.astype(jnp.bfloat16), AXES[0]).astype(jnp.float32),
+        lax.psum(d_self_o.astype(jnp.bfloat16), AXES[0]).astype(jnp.float32),
+        lax.psum(d_up.astype(jnp.bfloat16), AXES[0]).astype(jnp.float32),
+        lax.psum(d_upb.astype(jnp.bfloat16), AXES[0]).astype(jnp.float32),
+        lax.psum(d_down.astype(jnp.bfloat16), AXES[0]).astype(jnp.float32),
     )
     return (
         result,
@@ -387,45 +392,1060 @@
     )
 
 
+BF = jnp.bfloat16
+F32 = jnp.float32
+SCALE = HS ** (-0.5)
+SELF, KV, QO, DOWN, UP = "self", "kv", "qo", "down", "up"
+BIT_X, BIT_CORE, BIT_Y, BIT_Z0, BIT_Z1 = 1, 2, 4, 8, 16
+DEVICES = 32
+VMEM_LIMIT = 60 << 20
+
+
+def dg(left, right, left_dim, right_dim):
+    return lax.dot_general(
+        left, right, (((left_dim,), (right_dim,)), ((), ())), preferred_element_type=F32
+    )
+
+
+def swap(array, bit):
+    return lax.ppermute(array, AXES, [(i, i ^ bit) for i in range(DEVICES)])
+
+
+def total(terms, kind=BF):
+    out = terms[0].astype(F32)
+    for term in terms[1:]:
+        out = out + term.astype(F32)
+    return out.astype(kind)
+
+
+def call(body, name, grid, in_specs, out_specs, out_shape, scalars, operands, scratch=(), aliases=None, flops=0, moved=0):
+    spec = pltpu.PrefetchScalarGridSpec(
+        num_scalar_prefetch=1, grid=grid, in_specs=in_specs, out_specs=out_specs, scratch_shapes=list(scratch)
+    )
+    return pl.pallas_call(
+        body,
+        out_shape=out_shape,
+        grid_spec=spec,
+        input_output_aliases=aliases or {},
+        compiler_params=pltpu.CompilerParams(vmem_limit_bytes=VMEM_LIMIT),
+        cost_estimate=pl.CostEstimate(flops=int(flops), bytes_accessed=int(moved), transcendentals=0),
+        name=name,
+    )(scalars, *operands)
+
+
+def sds(shape, kind):
+    return jax.ShapeDtypeStruct(shape, kind)
+
+
+def own_quarters(name, groups, scalars, whole):
+    operands, specs, outs, shapes, plan = [], [], [], [], []
+    for weights, by_rows, part in groups:
+        rows, columns = weights[0].shape
+        first = len(operands)
+        for weight in weights:
+            operands.append(weight)
+            if by_rows:
+                specs.append(pl.BlockSpec((part, columns), lambda i, s: (i ^ s[0], 0)))
+            else:
+                specs.append(pl.BlockSpec((rows, part), lambda i, s: (0, i ^ s[0])))
+        plan.append((first, len(weights), by_rows, part))
+        count = 4 if whole else 1
+        if by_rows:
+            outs.append(pl.BlockSpec((len(weights) * part, columns), lambda i, s: (i, 0)))
+            shapes.append(sds((count * len(weights) * part, columns), BF))
+        else:
+            outs.append(pl.BlockSpec((rows, len(weights) * part), lambda i, s: (0, i)))
+            shapes.append(sds((rows, count * len(weights) * part), BF))
+
+    def body(scal_ref, *refs):
+        for n, (first, count, by_rows, part) in enumerate(plan):
+            out = refs[len(operands) + n]
+            for k in range(count):
+                cut = slice(k * part, (k + 1) * part)
+                if by_rows:
+                    out[cut, :] = refs[first + k][...]
+                else:
+                    out[:, cut] = refs[first + k][...]
+
+    return call(
+        body,
+        name,
+        (4 if whole else 1,),
+        specs,
+        outs,
+        shapes,
+        scalars,
+        operands,
+        moved=sum(shape.size for shape in shapes) * 4,
+    )
+
+
+def enter(name, values, gain, shift, weights, row_block):
+    rows, width = values.shape
+    count = len(weights)
+
+    def body(scal_ref, v_ref, gain_ref, shift_ref, *refs):
+        half = row_block // 2
+        for part in range(2):
+            cut = slice(part * half, (part + 1) * half)
+            v = v_ref[cut, :].astype(F32)
+            average = jnp.mean(v, axis=-1, keepdims=True)
+            centered = v - average
+            scale = lax.rsqrt(jnp.mean(centered * centered, axis=-1, keepdims=True) + EPSILON)
+            normed = (centered * scale * gain_ref[...] + shift_ref[...]).astype(BF)
+            refs[count][cut, :] = normed
+            for k in range(count):
+                refs[count + 1 + k][cut, :] = dg(normed, refs[k][...], 1, 0).astype(BF)
+
+    block = pl.BlockSpec((row_block, width), lambda i, s: (i, 0))
+    line = pl.BlockSpec((1, width), lambda i, s: (0, 0))
+    return call(
+        body,
+        name,
+        (rows // row_block,),
+        [block, line, line] + [pl.BlockSpec(w.shape, lambda i, s: (0, 0)) for w in weights],
+        [block] + [pl.BlockSpec((row_block, w.shape[1]), lambda i, s: (i, 0)) for w in weights],
+        [sds(values.shape, BF)] + [sds((rows, w.shape[1]), BF) for w in weights],
+        jnp.zeros((1,), jnp.int32),
+        [values, gain, shift, *weights],
+        flops=sum(2 * rows * w.size for w in weights),
+        moved=rows * width * 8,
+    )
+
+
+def block_of(weight):
+    array, rows, columns, row, column = weight
+    return pl.BlockSpec((rows, columns), lambda i, s: (row, column))
+
+
+def project(name, values, weights):
+    rows = values.shape[0]
+    columns = sum(w[2] for w in weights)
+
+    def body(scal_ref, x_ref, *refs):
+        start = 0
+        for n, w in enumerate(weights):
+            refs[-1][:, start : start + w[2]] = dg(x_ref[...], refs[n][...], 1, 0).astype(BF)
+            start += w[2]
+
+    return call(
+        body,
+        name,
+        (1,),
+        [pl.BlockSpec(values.shape, lambda i, s: (0, 0))] + [block_of(w) for w in weights],
+        pl.BlockSpec((rows, columns), lambda i, s: (0, 0)),
+        sds((rows, columns), BF),
+        jnp.zeros((1,), jnp.int32),
+        [values] + [w[0] for w in weights],
+        flops=2 * values.size * columns,
+        moved=(values.size + values.shape[1] * columns + rows * columns) * 2,
+    )
+
+
+def mix_norm(name, residual, mixed, weights, bias, gain, shift):
+    rows, width = residual.shape
+    operands = [residual, bias, gain, shift, *mixed] + [w[0] for w in weights]
+
+    def body(scal_ref, *refs):
+        stream_ref, normed_ref, whole = refs[-3:]
+        start = 0
+        for n, w in enumerate(weights):
+            whole[start : start + w[1], :] = refs[4 + len(mixed) + n][...]
+            start += w[1]
+        branch, start = None, 0
+        for n, m in enumerate(mixed):
+            term = dg(refs[4 + n][...], whole[start : start + m.shape[1], :], 1, 0)
+            branch = term if branch is None else branch + term
+            start += m.shape[1]
+        for at in range(0, rows, 128):
+            cut = slice(at, at + 128)
+            out = refs[0][cut, :].astype(F32) + refs[1][...] + branch[cut]
+            stream_ref[cut, :] = out
+            average = jnp.mean(out, axis=-1, keepdims=True)
+            centered = out - average
+            scale = lax.rsqrt(jnp.mean(centered * centered, axis=-1, keepdims=True) + EPSILON)
+            normed_ref[cut, :] = (centered * scale * refs[2][...] + refs[3][...]).astype(BF)
+
+    block = pl.BlockSpec((rows, width), lambda i, s: (0, 0))
+    line = pl.BlockSpec((1, width), lambda i, s: (0, 0))
+    total_rows = sum(w[1] for w in weights)
+    return call(
+        body,
+        name,
+        (1,),
+        [block, line, line, line]
+        + [pl.BlockSpec(m.shape, lambda i, s: (0, 0)) for m in mixed]
+        + [block_of(w) for w in weights],
+        [block, block, pl.BlockSpec((total_rows, width), lambda i, s: (0, 0))],
+        [sds((rows, width), F32), sds((rows, width), BF), sds((total_rows, width), BF)],
+        jnp.zeros((1,), jnp.int32),
+        operands,
+        flops=2 * rows * width * total_rows,
+        moved=rows * width * 12,
+    )
+
+
+def head(ref, at):
+    return ref[:, at * HS : (at + 1) * HS]
+
+
+def attend(name, arrays, heads_at, lengths, key_rows):
+    groups = lengths.shape[0]
+    heads = len(heads_at)
+    count = len(arrays)
+
+    def body(len_ref, *refs):
+        mixed_ref, lse_ref = refs[-2], refs[-1]
+        visible = lax.broadcasted_iota(jnp.int32, (key_rows, LAT), 0) < len_ref[pl.program_id(0)]
+        width = min(4, heads)
+        for first in range(0, heads, width):
+            some = heads_at[first : first + width]
+            scores = [dg(head(refs[k[0]], k[1]), head(refs[q[0]], q[1]), 1, 1) * SCALE for q, k, v in some]
+            scores = [jnp.where(visible, s, NEG_LARGE) for s in scores]
+            tops = [jnp.max(s, axis=0, keepdims=True) for s in scores]
+            exps = [jnp.exp(s - t) for s, t in zip(scores, tops)]
+            sums = [jnp.sum(e, axis=0, keepdims=True) for e in exps]
+            probs = [(e * (1.0 / s)).astype(BF) for e, s in zip(exps, sums)]
+            for n, (q, k, v) in enumerate(some):
+                h = first + n
+                mixed_ref[:, h * HS : (h + 1) * HS] = dg(probs[n], head(refs[v[0]], v[1]), 0, 0).astype(BF)
+                lse_ref[0, h : h + 1, :] = tops[n] + jnp.log(sums[n])
+
+    return call(
+        body,
+        name,
+        (groups,),
+        [pl.BlockSpec((LAT if q else key_rows, a.shape[1]), lambda i, s: (i, 0)) for a, q in arrays],
+        [pl.BlockSpec((LAT, heads * HS), lambda i, s: (i, 0)), pl.BlockSpec((1, 8, LAT), lambda i, s: (i, 0, 0))],
+        [sds((groups * LAT, heads * HS), BF), sds((groups, 8, LAT), F32)],
+        lengths,
+        [a for a, _ in arrays],
+        flops=groups * heads * key_rows * LAT * HS * 4,
+        moved=sum(a.size for a, _ in arrays) * 2,
+    )
+
+
+def attend_back(name, arrays, heads_at, d_mixed, totals, lengths, key_rows, outs, out_at):
+    groups = lengths.shape[0]
+    operands = [a for a, _ in arrays] + list(d_mixed[0]) + list(totals[0])
+    d_base = len(arrays)
+    l_base = d_base + len(d_mixed[0])
+    count = len(operands)
+    heads = len(heads_at)
+
+    def body(len_ref, *refs):
+        visible = lax.broadcasted_iota(jnp.int32, (key_rows, LAT), 0) < len_ref[pl.program_id(0)]
+        width = min(4, heads)
+
+        def put(spot, value):
+            refs[count + spot[0]][:, spot[1] * HS : (spot[1] + 1) * HS] = value.astype(BF)
+
+        for first in range(0, heads, width):
+            some = range(first, first + width)
+            q = [head(refs[heads_at[h][0][0]], heads_at[h][0][1]) for h in some]
+            k = [head(refs[heads_at[h][1][0]], heads_at[h][1][1]) for h in some]
+            v = [head(refs[heads_at[h][2][0]], heads_at[h][2][1]) for h in some]
+            d = [head(refs[d_base + d_mixed[1][h][0]], d_mixed[1][h][1]) for h in some]
+            logs = [refs[l_base + totals[1][h][0]][0, totals[1][h][1] : totals[1][h][1] + 1, :] for h in some]
+            scores = [dg(a, b, 1, 1) for a, b in zip(k, q)]
+            d_prob = [dg(a, b, 1, 1) for a, b in zip(v, d)]
+            probs = [jnp.exp(jnp.where(visible, s * SCALE, NEG_LARGE) - t) for s, t in zip(scores, logs)]
+            low_probs = [p.astype(BF) for p in probs]
+            inner = [jnp.sum(p * g, axis=0, keepdims=True) for p, g in zip(probs, d_prob)]
+            d_score = [(p * (g - i)).astype(BF) for p, g, i in zip(probs, d_prob, inner)]
+            for n, h in enumerate(some):
+                put(out_at[h][2], dg(low_probs[n], d[n], 1, 0))
+                put(out_at[h][1], dg(d_score[n], q[n], 1, 0) * SCALE)
+                put(out_at[h][0], dg(d_score[n], k[n], 0, 0) * SCALE)
+
+    return call(
+        body,
+        name,
+        (groups,),
+        [pl.BlockSpec((LAT if q else key_rows, a.shape[1]), lambda i, s: (i, 0)) for a, q in arrays]
+        + [pl.BlockSpec((LAT, a.shape[1]), lambda i, s: (i, 0)) for a in d_mixed[0]]
+        + [pl.BlockSpec((1, 8, LAT), lambda i, s: (i, 0, 0)) for _ in totals[0]],
+        [pl.BlockSpec((LAT if q else key_rows, n * HS), lambda i, s: (i, 0)) for q, n in outs],
+        [sds((groups * (LAT if q else key_rows), n * HS), BF) for q, n in outs],
+        lengths,
+        operands,
+        flops=groups * heads * key_rows * LAT * HS * 10,
+        moved=sum(a.size for a in operands) * 4,
+    )
+
+
+def mlp_block(x, g, up, bias, down):
+    cuts = [slice(at, at + 256) for at in range(0, up.shape[1], 256)]
+    pre = [dg(x, up[:, c], 1, 0) + bias[:, c] for c in cuts]
+    d_hidden = [dg(g, down[c, :], 1, 1) for c in cuts]
+    hidden, d_pre, sums = [], [], []
+    out = dx = None
+    for n, c in enumerate(cuts):
+        p = pre[n]
+        squared = p * p
+        tanh = jnp.tanh(p * (GELU_COEF + (GELU_COEF * GELU_CUBE) * squared))
+        half = 0.5 * (1.0 + tanh)
+        slope = half + (0.5 * p) * (1.0 - tanh * tanh) * (GELU_COEF + (3.0 * GELU_COEF * GELU_CUBE) * squared)
+        hid = (p * half).astype(BF)
+        d_wide = d_hidden[n] * slope
+        d = d_wide.astype(BF)
+        hidden.append(hid)
+        d_pre.append(d)
+        sums.append(jnp.sum(d_wide, axis=0, keepdims=True))
+        term, d_term = dg(hid, down[c, :], 1, 0), dg(d, up[:, c], 1, 1)
+        out = term if out is None else out + term
+        dx = d_term if dx is None else dx + d_term
+    return cuts, hidden, d_pre, sums, out, dx
+
+
+def mlp_pass(name, normed, grad, up, bias, down, scalars, kind):
+    rows, width = normed.shape
+    units = up.shape[1] // 4
+
+    def body(scal_ref, x_ref, g_ref, up_ref, b_ref, dn_ref, out_ref, dx_ref, h_ref, p_ref, db_ref, out_sum, dx_sum):
+        step = pl.program_id(0)
+        cuts, hidden, d_pre, sums, out, dx = mlp_block(x_ref[...], g_ref[...], up_ref, b_ref, dn_ref)
+        for n, c in enumerate(cuts):
+            h_ref[:, c] = hidden[n]
+            p_ref[:, c] = d_pre[n]
+            db_ref[:, c] = sums[n]
+        out_sum[...] = jnp.where(step == 0, 0.0, out_sum[...]) + out
+        dx_sum[...] = jnp.where(step == 0, 0.0, dx_sum[...]) + dx
+
+        @pl.when(step == 3)
+        def _():
+            out_ref[...] = out_sum[...].astype(kind)
+            dx_ref[...] = dx_sum[...].astype(kind)
+
+    fixed = pl.BlockSpec((rows, width), lambda i, s: (0, 0))
+    part = pl.BlockSpec((rows, units), lambda i, s: (0, i))
+    line = pl.BlockSpec((1, units), lambda i, s: (0, i))
+    return call(
+        body,
+        name,
+        (4,),
+        [
+            fixed,
+            fixed,
+            pl.BlockSpec((width, units), lambda i, s: (0, i)),
+            line,
+            pl.BlockSpec((units, width), lambda i, s: (i, 0)),
+        ],
+        [fixed, fixed, part, part, line],
+        [sds((rows, width), kind)] * 2 + [sds((rows, 4 * units), BF)] * 2 + [sds((1, 4 * units), F32)],
+        scalars,
+        [normed, grad, up, bias, down],
+        scratch=[pltpu.VMEM((rows, width), F32)] * 2,
+        flops=rows * width * units * 4 * 8,
+        moved=4 * rows * width * 4 + up.size * 4,
+    )
+
+
+def z_slot(row, z):
+    apart = row ^ z
+    return (apart & 1) * 2 + (apart >> 1)
+
+
+def mlp_grads(name, lefts, rights, scalars):
+    rows, width = lefts[0].shape
+    units = rights[0].shape[1] // 4
+    quarter = width // 4
+    count = len(lefts)
+
+    def body(scal_ref, *refs):
+        z = scal_ref[1]
+        out_ref = refs[-1]
+        product = None
+        for n in range(count):
+            term = dg(refs[n][...], refs[count + n][...], 0, 0)
+            product = term if product is None else product + term
+        for row in range(4):
+            out_ref[0, z_slot(row, z)] = product[row * quarter : (row + 1) * quarter].astype(BF)
+
+    return call(
+        body,
+        name,
+        (2,),
+        [pl.BlockSpec((rows, width), lambda i, s: (0, 0))] * count
+        + [pl.BlockSpec((rows, units), lambda i, s: (0, i ^ s[0]))] * count,
+        pl.BlockSpec((1, 4, quarter, units), lambda i, s: (i, 0, 0, 0)),
+        sds((2, 4, quarter, units), BF),
+        scalars,
+        [*lefts, *rights],
+        flops=2 * 2 * rows * width * units * count,
+        moved=4 * rows * width * count,
+    )
+
+
+def head_grads(name, pairs, scalars):
+    width = pairs[0][0].shape[1]
+    quarter = width // 4
+    counts = [pair[1].shape[1] // (8 * HS) for pair in pairs]
+    weights = sum(counts)
+
+    def body(scal_ref, *refs):
+        z = scal_ref[1]
+        keep_ref, send_ref = refs[-2], refs[-1]
+
+        def work(out_ref):
+            base = 0
+            for n, count in enumerate(counts):
+                product = dg(refs[2 * n][...], refs[2 * n + 1][...], 0, 0)
+                for row in range(4):
+                    slot = z_slot(row, z)
+                    for near in range(2):
+                        for w in range(count):
+                            at = (near * count + w) * HS
+                            out_ref[0, near, slot, base + w] = product[
+                                row * quarter : (row + 1) * quarter, at : at + HS
+                            ].astype(BF)
+                base += count
+
+        step = pl.program_id(0)
+
+        @pl.when(step < 2)
+        def _():
+            work(send_ref)
+
+        @pl.when(step >= 2)
+        def _():
+            work(keep_ref)
+
+    def column(i):
+        return (1 - i % 2) * 2 + (1 - i // 2)
+
+    def spot(i):
+        return (1 - i % 2, 0, 0, 0, 0, 0)
+
+    specs, operands = [], []
+    for (values, grads), count in zip(pairs, counts):
+        specs.append(pl.BlockSpec(values.shape, lambda i, s: (0, 0)))
+        specs.append(pl.BlockSpec((grads.shape[0], 2 * count * HS), lambda i, s: (0, column(i))))
+        operands += [values, grads]
+    shape = (2, 2, 4, weights, quarter, HS)
+    block = (1, 2, 4, weights, quarter, HS)
+    return call(
+        body,
+        name,
+        (4,),
+        specs,
+        [
+            pl.BlockSpec(block, lambda i, s: spot(jnp.maximum(i, 2))),
+            pl.BlockSpec(block, lambda i, s: spot(jnp.minimum(i, 1))),
+        ],
+        [sds(shape, BF)] * 2,
+        scalars,
+        operands,
+        flops=sum(2 * p[0].size * p[1].shape[1] for p in pairs),
+        moved=sum(p[0].size + p[1].size for p in pairs) * 2 + 8 * weights * width * HS * 2,
+    )
+
+
+class Sums:
+    def __init__(self, own, other):
+        self.terms, self.other, self.stage = list(own), other, 0 if other else 1
+        self.came = None
+
+    def step(self, line):
+        stage = self.stage
+        self.stage += 1
+
+        def view(held, at):
+            if at is None:
+                return held
+            for part in at:
+                held = held[part]
+            return held
+
+        def add(terms, cut):
+            return line(
+                lambda *held: total([view(h, t[1])[cut] for h, t in zip(held, terms)]), *[t[0] for t in terms]
+            )
+
+        if stage > 0 and stage < 4 and self.came is not None:
+            self.terms.append((self.came, ()))
+        if stage == 0:
+            self.came = swap(add(self.other, slice(None)), BIT_X)
+        elif stage == 1:
+            self.came = swap(add(self.terms, 1), BIT_Y)
+            self.terms = [(a, (*at, 0)) for a, at in self.terms]
+        elif stage == 2:
+            self.came = swap(add(self.terms, slice(2, 4)), BIT_Z0)
+            self.terms = [(a, (*at, slice(0, 2))) for a, at in self.terms]
+        elif stage == 3:
+            self.came = swap(add(self.terms, 1), BIT_Z1)
+            self.terms = [(a, (*at, 0)) for a, at in self.terms]
+        elif stage == 4:
+            self.piece = add(self.terms + [(self.came, ())], slice(None))
+            self.came = swap(self.piece, BIT_Z1)
+        elif stage == 5:
+            self.pair = line(lambda came, piece: jnp.stack([piece, came]), self.came, self.piece)
+            self.came = swap(self.pair, BIT_Z0)
+        elif stage == 6:
+            self.four = line(lambda came, pair: jnp.concatenate([pair, came], axis=0), self.came, self.pair)
+            self.near = swap(self.four, BIT_Y)
+            self.far = swap(self.four, BIT_CORE)
+        elif stage == 7:
+            near = line(lambda a: a, self.near)
+            self.quarters = [self.four, near, self.far, swap(near, BIT_CORE)]
+
+
+def finish(name, quarters, turned, scalars, shapes, column, held=()):
+    _, weights, quarter, units = quarters[0].shape
+    kept = len(held)
+
+    def body(scal_ref, *refs):
+        z = scal_ref[1]
+        outs = refs[4 + kept :]
+        step = pl.program_id(0)
+        for k in range(4):
+
+            @pl.when(step == k)
+            def _(k=k):
+                for row in range(4):
+                    slot = z_slot(row, z)
+                    for w in range(weights):
+                        block = refs[k][slot, w].astype(F32)
+                        rows = slice(row * quarter, (row + 1) * quarter)
+                        if turned[w]:
+                            outs[w][:, rows] = block.T
+                        else:
+                            outs[w][rows, :] = block
+
+    width = 4 * quarter
+    whole = pl.BlockSpec(quarters[0].shape, lambda i, s: (0, 0, 0, 0))
+    outs = [
+        pl.BlockSpec((units, width), lambda i, s: (column(i ^ s[0]), 0))
+        if turned[w]
+        else pl.BlockSpec((width, units), lambda i, s: (0, column(i ^ s[0])))
+        for w in range(weights)
+    ]
+    return call(
+        body,
+        name,
+        (4,),
+        [whole] * 4 + [pl.BlockSpec(memory_space=pl.ANY)] * kept,
+        outs,
+        [sds(shape, F32) for shape in shapes],
+        scalars,
+        [*quarters, *held],
+        aliases={1 + 4 + w: w for w in range(kept)},
+        moved=weights * width * units * 4 * 6,
+    )
+
+
+def norm_back(name, values, gain, given, products, residual, row_block=512):
+    rows, width = values.shape
+    operands = [values, gain, *given]
+    specs = [
+        pl.BlockSpec((row_block, width), lambda i, s: (i, 0)),
+        pl.BlockSpec((1, width), lambda i, s: (0, 0)),
+    ] + [pl.BlockSpec((row_block, width), lambda i, s: (i, 0))] * len(given)
+    spots = []
+    for grads, weights in products:
+        spots.append((len(operands), [w[2] for w in weights]))
+        operands.append(grads)
+        specs.append(pl.BlockSpec((row_block, grads.shape[1]), lambda i, s: (i, 0)))
+        for weight in weights:
+            operands.append(weight[0])
+            specs.append(block_of(weight))
+    if residual is not None:
+        operands.append(residual)
+        specs.append(pl.BlockSpec((row_block, width), lambda i, s: (i, 0)))
+    count = len(operands)
+
+    def body(scal_ref, *refs):
+        outs = refs[count:]
+        sums = outs[-1]
+        whole = None
+        for at, sizes in spots:
+            start = 0
+            for n, size in enumerate(sizes):
+                term = dg(refs[at][:, start : start + size], refs[at + 1 + n][...], 1, 1)
+                whole = term if whole is None else whole + term
+                start += size
+        column_sums = None
+        for at in range(0, row_block, 128):
+            cut = slice(at, at + 128)
+            d = None if whole is None else whole[cut]
+            for n in range(len(given)):
+                term = refs[2 + n][cut, :].astype(F32)
+                d = term if d is None else d + term
+            v = refs[0][cut, :].astype(F32)
+            average = jnp.mean(v, axis=-1, keepdims=True)
+            centered = v - average
+            scale = lax.rsqrt(jnp.mean(centered * centered, axis=-1, keepdims=True) + EPSILON)
+            unit = centered * scale
+            scaled = d * refs[1][...]
+            back = scale * (
+                scaled
+                - jnp.mean(scaled, axis=-1, keepdims=True)
+                - unit * jnp.mean(scaled * unit, axis=-1, keepdims=True)
+            )
+            if residual is not None:
+                back = back + refs[count - 1][cut, :].astype(F32)
+            outs[0][cut, :] = back
+            if residual is not None:
+                outs[1][cut, :] = back.astype(BF)
+            terms = [jnp.sum(t, axis=0, keepdims=True) for t in (d * unit, d, back)]
+            column_sums = terms if column_sums is None else [a + b for a, b in zip(column_sums, terms)]
+        first = pl.program_id(0) == 0
+        for n in range(3):
+            sums[n : n + 1, :] = jnp.where(first, 0.0, sums[n : n + 1, :]) + column_sums[n]
+
+    block = pl.BlockSpec((row_block, width), lambda i, s: (i, 0))
+    out_specs = [block] + [block] * (residual is not None) + [pl.BlockSpec((8, width), lambda i, s: (0, 0))]
+    out_shape = [sds((rows, width), F32)] + [sds((rows, width), BF)] * (residual is not None) + [sds((8, width), F32)]
+    return call(
+        body,
+        name,
+        (rows // row_block,),
+        specs,
+        out_specs,
+        out_shape,
+        jnp.zeros((1,), jnp.int32),
+        operands,
+        flops=sum(2 * g.size * width for g, _ in products),
+        moved=rows * width * 12,
+    )
+
+
+def row_shards(
+    latents,
+    inputs,
+    frames,
+    group_clip,
+    norm_gain,
+    norm_bias,
+    cross_q,
+    cross_k,
+    cross_v,
+    cross_o,
+    self_q,
+    self_k,
+    self_v,
+    self_o,
+    mlp_up,
+    up_bias,
+    mlp_down,
+    out_bias,
+    cotangent,
+):
+    dp = lax.axis_index(AXES[0])
+    core, near, z = dp & 1, (dp >> 1) & 1, dp >> 2
+    mine = 2 * core + near
+    scalars = jnp.stack([mine, z]).astype(jnp.int32)
+    own_groups = latents.shape[0] // LAT
+    key_rows = inputs.shape[0] // own_groups
+
+    width = latents.shape[1]
+    units = mlp_up.shape[1] // 4
+    last = [scalars]
+
+    def line(work, *args):
+        first, _ = lax.optimization_barrier((args[0], last[0]))
+        out = work(first, *args[1:])
+        last[0] = jax.tree.leaves(out)[0]
+        return out
+
+    def low_matmul(left, right):
+        return matmul(left, right).astype(BF)
+
+    def low_turned(left, right):
+        return times_transposed(left, right).astype(BF)
+
+    def settle(array):
+        last[0], out = lax.optimization_barrier((last[0], array))
+        return out
+
+    class Fetch:
+        def __init__(self, piece):
+            self.quarters = [swap(piece, BIT_X), None, None, None]
+
+        def near(self):
+            q = self.quarters
+            q[0] = settle(q[0])
+            q[1], q[2] = swap(q[0], BIT_Y), swap(q[0], BIT_CORE)
+
+        def far(self):
+            q = self.quarters
+            q[1] = settle(q[1])
+            q[3] = swap(q[1], BIT_CORE)
+
+    matches = group_clip[:, None] == lax.broadcasted_iota(jnp.int32, (1, frames.shape[0]), 1)
+    lengths = jnp.sum(jnp.where(matches, frames[None, :], 0), axis=1) * FRAME_ROWS
+    lengths = lax.dynamic_slice_in_dim(lengths, lax.axis_index(AXES[1]) * own_groups, own_groups, 0)
+    lengths = lengths.astype(jnp.int32)
+    full = jnp.full((own_groups,), LAT, jnp.int32)
+    gains = [norm_gain[n : n + 1] for n in range(4)]
+    shifts = [norm_bias[n : n + 1] for n in range(4)]
+
+    kv_near, q_near, o_near, s_near = line(
+        lambda s: own_quarters(
+            "pieces",
+            [
+                ([cross_k, cross_v], False, HS),
+                ([cross_q], False, HS),
+                ([cross_o, self_o], True, HS),
+                ([self_q, self_k, self_v], False, HS),
+            ],
+            s,
+            False,
+        ),
+        scalars,
+    )
+    kv, q, o, s3 = Fetch(kv_near), Fetch(q_near), Fetch(o_near), Fetch(s_near)
+    own_bias = up_bias.astype(F32)[None]
+    low3 = cotangent
+    low3_core = swap(low3, BIT_CORE)
+
+    (kv_own,) = line(lambda s: own_quarters("own_kv", [([cross_k, cross_v], False, HS)], s, True), scalars)
+    in_normed, keyval_own = line(
+        lambda x: enter("enter_inputs", x, gains[1], shifts[1], [kv_own], 512), inputs
+    )
+    kv.near()
+    low3_x = swap(low3, BIT_X)
+    q_own, o_own, s_own = line(
+        lambda s: own_quarters(
+            "own_rest",
+            [([cross_q], False, HS), ([cross_o, self_o], True, HS), ([self_q, self_k, self_v], False, HS)],
+            s,
+            True,
+        ),
+        scalars,
+    )
+    q.near()
+    lat_normed, query_own = line(lambda x: enter("enter_latents", x, gains[0], shifts[0], [q_own], 512), latents)
+    kv.far()
+    mixed_own, total_own = line(
+        lambda q: attend(
+            "cross_own",
+            [(q, True), (keyval_own, False)],
+            [((0, j), (1, 2 * j), (1, 2 * j + 1)) for j in range(4)],
+            lengths,
+            key_rows,
+        ),
+        query_own,
+    )
+    q.far()
+    o.near()
+    keyval_other = [None] * 4
+    for j in (0, 2, 1, 3):
+        keyval_other[j] = line(lambda w: low_matmul(in_normed, w), kv.quarters[j])
+    o.far()
+    query_other = line(
+        lambda x: project("query_other", x, [(w, width, HS, 0, 0) for w in q.quarters]), lat_normed
+    )
+    mixed_other, total_other = line(
+        lambda q: attend(
+            "cross_other",
+            [(q, True)] + [(a, False) for a in keyval_other],
+            [((0, j), (1 + j, 0), (1 + j, 1)) for j in range(4)],
+            lengths,
+            key_rows,
+        ),
+        query_other,
+    )
+    s3.near()
+    stream1, self_normed, co = line(
+        lambda m: mix_norm(
+            "mix_norm1",
+            latents,
+            [m, mixed_other],
+            [(o_own, HS, width, 2 * j, 0) for j in range(4)] + [(w, HS, width, 0, 0) for w in o.quarters],
+            out_bias[0:1],
+            gains[2],
+            shifts[2],
+        ),
+        mixed_own,
+    )
+    s3.far()
+    qkv = line(
+        lambda x: project(
+            "qkv", x, [(s_own, width, 12 * HS, 0, 0)] + [(w, width, 3 * HS, 0, 0) for w in s3.quarters]
+        ),
+        self_normed,
+    )
+    self_heads = [((0, 3 * j), (0, 3 * j + 1), (0, 3 * j + 2)) for j in range(8)]
+    smix, stotal = line(lambda q: attend("self", [(q, True)], self_heads, full, LAT), qkv)
+    stream2, mlp_normed, so = line(
+        lambda m: mix_norm(
+            "mix_norm2",
+            stream1,
+            [m],
+            [(o_own, HS, width, 2 * j + 1, 0) for j in range(4)] + [(w, HS, width, 1, 0) for w in o.quarters],
+            out_bias[1:2],
+            gains[3],
+            shifts[3],
+        ),
+        smix,
+    )
+
+    mlp_x, mlp_core = swap(mlp_normed, BIT_X), swap(mlp_normed, BIT_CORE)
+    low3_x = settle(low3_x)
+    low3_x_core = swap(low3_x, BIT_CORE)
+    out_own, dx_own, h_own, p_own, db_own = line(
+        lambda x: mlp_pass("mlp_own", x, low3, mlp_up, own_bias, mlp_down, scalars, F32), mlp_normed
+    )
+    h_core, p_core = swap(h_own, BIT_CORE), swap(p_own, BIT_CORE)
+    out_send, dx_send, h_x, p_x, db_x = line(
+        lambda x: mlp_pass("mlp_x", x, low3_x, mlp_up, own_bias, mlp_down, scalars, BF), mlp_x
+    )
+    dx_came = swap(dx_send, BIT_X)
+    h_x_core, p_x_core = swap(h_x, BIT_CORE), swap(p_x, BIT_CORE)
+    mlp_x_core = swap(mlp_x, BIT_CORE)
+    out_came = swap(out_send, BIT_X)
+
+    v, pieces, done = SimpleNamespace(), {}, {}
+
+    def norm_back3():
+        v.grad2, v.low2, v.sums3 = line(
+            lambda d: norm_back("norm_back3", stream2, gains[3], [d, dx_came], [], cotangent), dx_own
+        )
+
+    def down_grads():
+        piece = line(
+            lambda g: mlp_grads(
+                "down_grads", [g, low3_x, low3_core, low3_x_core], [h_own, h_x, h_core, h_x_core], scalars
+            ),
+            low3,
+        )
+        pieces[DOWN] = Sums([(piece, ())], [])
+
+    def up_grads():
+        piece = line(
+            lambda x: mlp_grads("up_grads", [x, mlp_x, mlp_core, mlp_x_core], [p_own, p_x, p_core, p_x_core], scalars),
+            mlp_normed,
+        )
+        pieces[UP] = Sums([(piece, ())], [])
+
+    def self_back():
+        d_smix = line(low_turned, v.low2, so)
+        (v.d_qkv,) = line(
+            lambda q: attend_back(
+                "self_back",
+                [(q, True)],
+                self_heads,
+                ((d_smix,), [(0, j) for j in range(8)]),
+                ((stotal,), [(0, j) for j in range(8)]),
+                full,
+                LAT,
+                [(True, 24)],
+                self_heads,
+            ),
+            qkv,
+        )
+
+    def self_grads():
+        keep, send = line(
+            lambda x: head_grads("self_grads", [(x, v.d_qkv), (v.low2, smix)], scalars), self_normed
+        )
+        came = swap(send, BIT_CORE)
+        pieces[SELF] = Sums([(keep, (0,)), (came, (0,))], [(keep, (1,)), (came, (1,))])
+
+    def norm_back2():
+        v.grad1, v.low1, v.sums2 = line(
+            lambda d: norm_back("norm_back2", stream1, gains[2], [], [(d, [(s_own, width, 12 * HS, 0, 0)] + [(w, width, 3 * HS, 0, 0) for w in s3.quarters])], v.grad2),
+            v.d_qkv,
+        )
+
+    def cross_back():
+        d_mix = line(low_turned, v.low1, co)
+        v.d_query, v.d_keyval = line(
+            lambda q: attend_back(
+                "cross_back",
+                [(q, True), (query_other, True), (keyval_own, False)] + [(a, False) for a in keyval_other],
+                [((0, j), (2, 2 * j), (2, 2 * j + 1)) for j in range(4)]
+                + [((1, j), (3 + j, 0), (3 + j, 1)) for j in range(4)],
+                ((d_mix,), [(0, j) for j in range(8)]),
+                ((total_own, total_other), [(j // 4, j % 4) for j in range(8)]),
+                lengths,
+                key_rows,
+                [(True, 8), (False, 16)],
+                [((0, j), (1, 2 * j), (1, 2 * j + 1)) for j in range(8)],
+            ),
+            query_own,
+        )
+
+    def kv_grads():
+        keep, send = line(lambda x: head_grads("kv_grads", [(x, v.d_keyval)], scalars), in_normed)
+        came = swap(send, BIT_CORE)
+        pieces[KV] = Sums([(keep, (0,)), (came, (0,))], [(keep, (1,)), (came, (1,))])
+
+    def q_grads():
+        mix = line(lambda a, b: jnp.concatenate([a, b], axis=1), mixed_own, mixed_other)
+        keep, send = line(
+            lambda x: head_grads("q_grads", [(x, v.d_query), (v.low1, mix)], scalars), lat_normed
+        )
+        came = swap(send, BIT_CORE)
+        pieces[QO] = Sums([(keep, (0,)), (came, (0,))], [(keep, (1,)), (came, (1,))])
+
+    def norm_back1():
+        v.d_inputs, v.sums1 = line(
+            lambda d: norm_back("norm_back1", inputs, gains[1], [], [(d, [(kv_own, width, 8 * HS, 0, 0)] + [(w, width, 2 * HS, 0, 0) for w in kv.quarters])], None),
+            v.d_keyval,
+        )
+
+    def norm_back0():
+        v.d_latents, _, v.sums0 = line(
+            lambda d: norm_back("norm_back0", latents, gains[0], [], [(d, [(q_own, width, 4 * HS, 0, 0)] + [(w, width, HS, 0, 0) for w in q.quarters])], v.grad1),
+            v.d_query,
+        )
+
+    def result():
+        v.result = line(
+            lambda a: (stream2 + (a + out_came.astype(F32)) + out_bias[2]).astype(BF),
+            out_own,
+        )
+
+    def small():
+        every = [v.sums0, v.sums1, v.sums2, v.sums3]
+        shared = [a[0] for a in every] + [a[1] for a in every]
+        shared += [v.sums2[2], v.sums3[2], jnp.sum(cotangent.astype(F32), axis=0)]
+        v.small = line(lambda a, *rest: jnp.stack([a, *rest]), *shared)
+
+    def small_x():
+        units_sums = (db_own + db_x).reshape(-1, width)
+        v.small = line(
+            lambda a, b, c: jnp.concatenate([a + b, c], axis=0), v.small, swap(v.small, BIT_X), units_sums
+        )
+
+    def small_step(bit):
+        def run():
+            v.small = line(lambda a, b: a + b, v.small, swap(v.small, bit))
+
+        return run
+
+    def finish_heads(key, turned, shapes):
+        def run():
+            done[key] = line(
+                lambda f: finish(
+                    key + "_finish", [f, *pieces[key].quarters[1:]], turned, scalars, shapes, lambda q: q
+                ),
+                pieces[key].quarters[0],
+            )
+
+        return run
+
+    def finish_mlp(key, turned, shape):
+        def run():
+            done[key] = line(
+                lambda f: finish(
+                    key + "_finish",
+                    [q[:, None] for q in [f, *pieces[key].quarters[1:]]],
+                    [turned],
+                    scalars,
+                    [shape],
+                    lambda q: q,
+                ),
+                pieces[key].quarters[0],
+            )
+
+        return run
+
+    order = (
+        down_grads,
+        up_grads,
+        DOWN,
+        norm_back3,
+        self_back,
+        self_grads,
+        UP,
+        norm_back2,
+        SELF,
+        DOWN,
+        cross_back,
+        DOWN,
+        UP,
+        kv_grads,
+        DOWN,
+        UP,
+        KV,
+        q_grads,
+        DOWN,
+        UP,
+        QO,
+        SELF,
+        DOWN,
+        UP,
+        norm_back1,
+        UP,
+        SELF,
+        DOWN,
+        norm_back0,
+        small,
+        UP,
+        SELF,
+        KV,
+        result,
+        small_x,
+        SELF,
+        KV,
+        QO,
+        small_step(BIT_CORE),
+        finish_mlp(DOWN, True, mlp_down.shape),
+        SELF,
+        KV,
+        QO,
+        small_step(BIT_Y),
+        finish_mlp(UP, False, mlp_up.shape),
+        SELF,
+        KV,
+        QO,
+        small_step(BIT_Z0),
+        KV,
+        QO,
+        small_step(BIT_Z1),
+        SELF,
+        KV,
+        QO,
+        finish_heads(SELF, [False] * 3 + [True], [cross_q.shape] * 3 + [cross_o.shape]),
+        KV,
+        QO,
+        finish_heads(KV, [False] * 2, [cross_q.shape] * 2),
+        QO,
+        finish_heads(QO, [False, True], [cross_q.shape, cross_o.shape]),
+    )
+    for work in order:
+        if isinstance(work, str):
+            pieces[work].step(line)
+        else:
+            work()
+    d_self_q, d_self_k, d_self_v, d_self_o = done[SELF]
+    d_cross_k, d_cross_v = done[KV]
+    d_cross_q, d_cross_o = done[QO]
+    sums = v.small
+    return (
+        v.result,
+        v.d_latents,
+        v.d_inputs,
+        sums[0:4],
+        sums[4:8],
+        sums[8:11],
+        d_cross_q,
+        d_cross_k,
+        d_cross_v,
+        d_cross_o,
+        d_self_q,
+        d_self_k,
+        d_self_v,
+        d_self_o,
+        done[UP][0],
+        sums[11:].reshape(-1),
+        done[DOWN][0],
+    )
+
+
 def solution(mesh):
+    rows, columns, heads, whole = P(AXES, None), P(None, AXES[1]), P(AXES[1], None), P()
     in_specs = (
-        P(("dp", "tensor"), None),
-        P(("dp", "tensor"), None),
-        P(),
-        P("dp"),
-        P(),
-        P(),
-        P(None, "tensor"),
-        P(None, "tensor"),
-        P(None, "tensor"),
-        P("tensor", None),
-        P(None, "tensor"),
-        P(None, "tensor"),
-        P(None, "tensor"),
-        P("tensor", None),
-        P(None, "tensor"),
-        P("tensor"),
-        P("tensor", None),
-        P(),
-        P(("dp", "tensor"), None),
+        rows, rows, whole, P(AXES[0]), whole, whole, columns, columns, columns, heads, columns, columns, columns, heads,
+        columns, P(AXES[1]), heads, whole, rows,
     )
     out_specs = (
-        P(("dp", "tensor"), None),
-        P(("dp", "tensor"), None),
-        P(("dp", "tensor"), None),
-        P(),
-        P(),
-        P(),
-        P(None, "tensor"),
-        P(None, "tensor"),
-        P(None, "tensor"),
-        P("tensor", None),
-        P(None, "tensor"),
-        P(None, "tensor"),
-        P(None, "tensor"),
-        P("tensor", None),
-        P(None, "tensor"),
-        P("tensor"),
-        P("tensor", None),
-    )
+        rows, rows, rows, whole, whole, whole, columns, columns, columns, heads, columns, columns, columns, heads,
+        columns, P(AXES[1]), heads,
+    )
+    paired = mesh.shape[AXES[0]] == 16 and mesh.shape[AXES[1]] == 2
+    shards = row_shards if paired else split_shards
     return jax.shard_map(shards, mesh=mesh, in_specs=in_specs, out_specs=out_specs, check_vma=False)

time: 1350 us -> 594 us (0.44)
  waiting for transfers between devices: 786 us -> 182 us
  Pallas kernels: 0 us -> 250 us
  matrix products: 230 us -> 20.7 us
  local copies, waits for them, and re-layouts: 137 us -> 22.5 us
  blocking collectives: 76.1 us -> 0 us
  starting transfers between devices: 2.65 us -> 60 us
  other arithmetic: 93.8 us -> 47.2 us
    reduce_scatter x7 -> x0, waiting for transfers between devices: 279 us -> none  [the longest x3 162 us: branch_sum(): lax.psum_scatter(term(jnp.int32(0), lax.axis_size('tensor') * own_rows),...]
    all_gather x7 -> x0, waiting for transfers between devices: 256 us -> none  [the longest x1 102 us: shards(): lax.all_gather(in_normed, 'tensor', axis=0, tiled=True)]
    pallas_call x0 -> x30, Pallas kernels: none -> 250 us  [call(): pl.pallas_call(body, out_shape=out_shape, grid_spec=spec, input_output_al...]
    psum x1 -> x0, waiting for transfers between devices: 250 us -> none  [shards(): lax.psum(d_cross_q.astype(jnp.bfloat16), 'dp').astype(jnp.float32)]
    ppermute x0 -> x79, waiting for transfers between devices: none -> 182 us  [swap(): return lax.ppermute(array, AXES, [(i, i ^ bit) for i in range(DEVICES)])]
    dot_general x40 -> x0, matrix products: 99.5 us -> none  [the longest x10 52 us: gram_left(): lax.dot_general(left, right, (((0,), (0,)), ((), ())), preferred_element_...]
    psum x2 -> x0, blocking collectives: 76.1 us -> none  [the longest x1 40.3 us: shards(): lax.psum((gain_grads, shift_grads, bias_grads), ('dp', 'tensor'))]
    ppermute x0 -> x79, starting transfers between devices: none -> 60 us  [swap(): return lax.ppermute(array, AXES, [(i, i ^ bit) for i in range(DEVICES)])]
  transfers between devices with their start and end apart: 15 -> 79, of which waited for: 14 -> 30; matrix products, arithmetic and copies ran while one was open for 11% -> 12% of each run, Pallas kernels for 0% -> 33%
where the time goes in v1:
time: 594 us; the launch traced here: 584 us
  Pallas kernels  250 us (42%)
  waiting for transfers between devices  182 us (31%)
  starting transfers between devices  60 us (10%)
  other arithmetic  47.2 us (8%)
  local copies, waits for them, and re-layouts  22.5 us (4%)
  matrix products  20.7 us (3%)
    pallas_call x30, Pallas kernels, call(): pl.pallas_call(body, out_shape=out_shape, grid_spec=spec, input_output_al...  250 us
    ppermute x79, waiting for transfers between devices, swap(): return lax.ppermute(array, AXES, [(i, i ^ bit) for i in range(DEVICES)])  182 us
    ppermute x79, starting transfers between devices, swap(): return lax.ppermute(array, AXES, [(i, i ^ bit) for i in range(DEVICES)])  60 us
    convert_element_type x21, other arithmetic, total(): return out.astype(kind)  36.6 us
    dot_general x4, matrix products, matmul(): return jnp.dot(left, right, preferred_element_type=jnp.float32)  14.9 us
    unnamed x123, local copies, waits for them, and re-layouts  12.6 us
  transfers between devices with their start and end apart: 79, of which 30 were waited for; matrix products, arithmetic and copies ran while one was open for 12% of the time, Pallas kernels for 33%

profile of v1, /device:TPU:0, one launch (start us, length us, event | category | flops | bytes accessed | tf_op | source)
XLA Modules:
  0.0 584.1 jit_solution(3054947759762888993)
XLA Ops:
  15.9 9.5 %enter_inputs.1 = (bf16[2048,1024]{1,0:T(8,128)(2,1)}, bf16[2048,1024]{1,0:T(8,128)(2,1)}) custom-call(s32[1]{0:T(128)} %constant.11.clone.1.scal_ref, bf16[2048,1024]{1,0:T(8,128)(2,1)} %refs_0_.11, f32[1,1024]{1,0:T(1,128)} %get-tuple-element.321.gain_ref.refs_1_, f32[1,1024]{1,0:T(1,128)} %get-tuple-element.317.shift_ref, ...), custom_call_target="tpu_custom_call" | custom-call | flops 4294967296 | bytes 16777216 | tf_op jit(solution)/shard_map/enter_inputs/pallas_call | solution.py:425
  89.7 10.0 %collective-permute-done.13.refs_2_.refs_5_ = bf16[1024,384]{1,0:T(8,128)(2,1)} collective-permute-done((bf16[1024,384]{1,0:T(8,128)(2,1)S(1)}, bf16[1024,384]{1,0:T(8,128)(2,1)}, u32[]{:S(2)}, u32[]{:S(2)}) %collective-permute-start.13) | collective-permute-done | bytes 786464 | tf_op jit(solution)/shard_map/ppermute | solution.py:411
  103.1 8.7 %qkv.1.refs_0_ = bf16[512,3072]{1,0:T(8,128)(2,1)} custom-call(s32[1]{0:T(128)} %constant.11.clone.1.scal_ref, bf16[512,1024]{1,0:T(8,128)(2,1)} %get-tuple-element.212.x_ref.refs_0_, bf16[1024,1536]{1,0:T(8,128)(2,1)} %get-tuple-element.183.refs_0_.refs_3_, bf16[1024,384]{1,0:T(8,128)(2,1)} %copy-done.30, ...), custom_call_target="tpu_custom_call" | custom-call | flops 3221225472 | bytes 10485760 | tf_op jit(solution)/shard_map/qkv/pallas_call | solution.py:425
  126.8 16.0 %mlp_own.1 = (f32[512,1024]{1,0:T(8,128)}, f32[512,1024]{1,0:T(8,128)}, bf16[512,2048]{1,0:T(8,128)(2,1)}, bf16[512,2048]{1,0:T(8,128)(2,1)}, f32[1,2048]{1,0:T(1,128)}) custom-call(s32[2]{0:T(128)} %pad_add_fusion.scal_ref, bf16[512,1024]{1,0:T(8,128)(2,1)} %get-tuple-element.199.x_ref.refs_0_, bf16[512,1024]{1,0:T(8,128)(2,1)} %refs_4_.5, ...), custom_call_target="tpu_custom_call" | custom-call | flops 8589934592 | bytes 16777216 | tf_op jit(solution)/shard_map/mlp_own/pallas_call | solution.py:425
  150.2 15.7 %mlp_x.1 = (bf16[512,1024]{1,0:T(8,128)(2,1)}, bf16[512,1024]{1,0:T(8,128)(2,1)}, bf16[512,2048]{1,0:T(8,128)(2,1)}, bf16[512,2048]{1,0:T(8,128)(2,1)}, f32[1,2048]{1,0:T(1,128)}) custom-call(s32[2]{0:T(128)} %pad_add_fusion.scal_ref, bf16[512,1024]{1,0:T(8,128)(2,1)} %collective-permute-done.16.x_ref.refs_1_, bf16[512,1024]{1,0:T(8,128)(2,1)} %copy-done.53, ...), custom_call_target="tpu_custom_call" | custom-call | flops 8589934592 | bytes 16777216 | tf_op jit(solution)/shard_map/mlp_x/pallas_call | solution.py:425
  176.3 9.4 %down_grads.1 = bf16[2,4,256,512]{3,2,1,0:T(8,128)(2,1)} custom-call(s32[2]{0:T(128)} %pad_add_fusion.scal_ref, bf16[512,1024]{1,0:T(8,128)(2,1)} %refs_4_.5, bf16[512,1024]{1,0:T(8,128)(2,1)} %copy-done.53, bf16[512,1024]{1,0:T(8,128)(2,1)} %collective-permute-done.18.refs_2_, bf16[512,1024]{1,0:T(8,128)(2,1)} %copy-done.54, ...), custom_call_target="tpu_custom_call" | custom-call | flops 4294967296 | bytes 8388608 | tf_op jit(solution)/shard_map/down_grads/pallas_call | solution.py:425
  185.8 9.6 %up_grads.1 = bf16[2,4,256,512]{3,2,1,0:T(8,128)(2,1)} custom-call(s32[2]{0:T(128)} %pad_add_fusion.scal_ref, bf16[512,1024]{1,0:T(8,128)(2,1)} %get-tuple-element.199.x_ref.refs_0_, bf16[512,1024]{1,0:T(8,128)(2,1)} %collective-permute-done.16.x_ref.refs_1_, bf16[512,1024]{1,0:T(8,128)(2,1)} %collective-permute-done.22.refs_2_, ...), custom_call_target="tpu_custom_call" | custom-call | flops 4294967296 | bytes 8388608 | tf_op jit(solution)/shard_map/up_grads/pallas_call | solution.py:425
  211.1 7.3 %self_back.1.refs_1_.refs_2_ = bf16[512,3072]{1,0:T(8,128)(2,1)} custom-call(s32[4]{0:T(128)} %broadcast_2_len_ref.2.len_ref, bf16[512,3072]{1,0:T(8,128)(2,1)} %qkv.1.refs_0_, bf16[512,1024]{1,0:T(8,128)(2,1)} %convolution_convert_fusion.5.refs_1_, f32[4,8,128]{2,1,0:T(8,128)} %get-tuple-element.211.refs_2_), custom_call_target="tpu_custom_call" | custom-call | flops 671088640 | bytes 8404992 | tf_op jit(solution)/shard_map/self_back/pallas_call | solution.py:425
  218.4 11.2 %self_grads.1 = (bf16[2,2,4,4,256,128]{5,4,3,2,1,0:T(8,128)(2,1)}, bf16[2,2,4,4,256,128]{5,4,3,2,1,0:T(8,128)(2,1)}) custom-call(s32[2]{0:T(128)} %pad_add_fusion.scal_ref, bf16[512,1024]{1,0:T(8,128)(2,1)} %get-tuple-element.212.x_ref.refs_0_, bf16[512,3072]{1,0:T(8,128)(2,1)} %self_back.1.refs_1_.refs_2_, bf16[512,1024]{1,0:T(8,128)(2,1)} %get-tuple-element.208.refs_2_, ...), custom_call_target="tpu_custom_call" | custom-call | flops 4294967296 | bytes 14680064 | tf_op jit(solution)/shard_map/self_grads/pallas_call | solution.py:425
  232.8 11.6 %norm_back2.1 = (f32[512,1024]{1,0:T(8,128)}, bf16[512,1024]{1,0:T(8,128)(2,1)}, f32[8,1024]{1,0:T(8,128)}) custom-call(s32[1]{0:T(128)} %constant.11.clone.1.scal_ref, f32[512,1024]{1,0:T(8,128)} %get-tuple-element.181.refs_0_, f32[1,1024]{1,0:T(1,128)} %get-tuple-element.320.refs_2_.refs_1_, bf16[512,3072]{1,0:T(8,128)(2,1)} %self_back.1.refs_1_.refs_2_, ...), custom_call_target="tpu_custom_call" | custom-call | flops 3221225472 | bytes 6291456 | tf_op jit(solution)/shard_map/norm_back2/pallas_call | solution.py:425
  247.5 8.5 %collective-permute-done.28 = bf16[4,256,512]{2,1,0:T(8,128)(2,1)} collective-permute-done((bf16[4,256,512]{2,1,0:T(8,128)(2,1)}, bf16[4,256,512]{2,1,0:T(8,128)(2,1)}, u32[]{:S(2)}, u32[]{:S(2)}) %collective-permute-start.28) | collective-permute-done | bytes 1048608 | tf_op jit(solution)/shard_map/ppermute | solution.py:411
  261.3 12.5 %cross_back.1 = (bf16[512,1024]{1,0:T(8,128)(2,1)}, bf16[2048,2048]{1,0:T(8,128)(2,1)}) custom-call(s32[4]{0:T(128)} %dynamic_slice.3.len_ref, bf16[512,512]{1,0:T(8,128)(2,1)} %get-tuple-element.223.refs_0_, bf16[512,512]{1,0:T(8,128)(2,1)} %query_other.1.refs_0_.refs_1_, bf16[2048,1024]{1,0:T(8,128)(2,1)} %get-tuple-element.164.refs_1_.refs_2_, ...), custom_call_target="tpu_custom_call" | custom-call | flops 2684354560 | bytes 21004288 | tf_op jit(solution)/shard_map/cross_back/pallas_call | solution.py:425
  279.4 14.8 %kv_grads.1 = (bf16[2,2,4,2,256,128]{5,4,3,2,1,0:T(8,128)(2,1)}, bf16[2,2,4,2,256,128]{5,4,3,2,1,0:T(8,128)(2,1)}) custom-call(s32[2]{0:T(128)} %pad_add_fusion.scal_ref, bf16[2048,1024]{1,0:T(8,128)(2,1)} %get-tuple-element.229.refs_0_, bf16[2048,2048]{1,0:T(8,128)(2,1)} %get-tuple-element.246.refs_1_.refs_2_), custom_call_target="tpu_custom_call" | custom-call | flops 8589934592 | bytes 16777216 | tf_op jit(solution)/shard_map/kv_grads/pallas_call | solution.py:425
  298.5 14.8 %collective-permute-done.31 = bf16[256,512]{1,0:T(8,128)(2,1)S(1)} collective-permute-done((bf16[256,512]{1,0:T(8,128)(2,1)S(1)}, bf16[256,512]{1,0:T(8,128)(2,1)S(1)}, u32[]{:S(2)}, u32[]{:S(2)}) %collective-permute-start.31) | collective-permute-done | bytes 262176 | tf_op jit(solution)/shard_map/ppermute | solution.py:411
  319.5 7.8 %q_grads.1 = (bf16[2,2,4,2,256,128]{5,4,3,2,1,0:T(8,128)(2,1)}, bf16[2,2,4,2,256,128]{5,4,3,2,1,0:T(8,128)(2,1)}) custom-call(s32[2]{0:T(128)} %pad_add_fusion.scal_ref, bf16[512,1024]{1,0:T(8,128)(2,1)} %get-tuple-element.237.x_ref.refs_0_, bf16[512,1024]{1,0:T(8,128)(2,1)} %get-tuple-element.251.refs_1_.refs_2_, ...), custom_call_target="tpu_custom_call" | custom-call | flops 2147483648 | bytes 8388608 | tf_op jit(solution)/shard_map/q_grads/pallas_call | solution.py:425
  333.1 17.6 %collective-permute-done.32 = bf16[256,512]{1,0:T(8,128)(2,1)} collective-permute-done((bf16[256,512]{1,0:T(8,128)(2,1)S(1)}, bf16[256,512]{1,0:T(8,128)(2,1)}, u32[]{:S(2)}, u32[]{:S(2)}) %collective-permute-start.32) | collective-permute-done | bytes 262176 | tf_op jit(solution)/shard_map/ppermute | solution.py:411
  359.8 16.1 %collective-permute-done.39 = bf16[2,4,4,256,128]{4,3,2,1,0:T(8,128)(2,1)} collective-permute-done((bf16[2,4,4,256,128]{4,3,2,1,0:T(8,128)(2,1)S(1)}, bf16[2,4,4,256,128]{4,3,2,1,0:T(8,128)(2,1)}, u32[]{:S(2)}, u32[]{:S(2)}) %collective-permute-start.39) | collective-permute-done | bytes 2097184 | tf_op jit(solution)/shard_map/ppermute | solution.py:411
  386.0 18.7 %norm_back1.1 = (f32[2048,1024]{1,0:T(8,128)}, f32[8,1024]{1,0:T(8,128)}) custom-call(s32[1]{0:T(128)} %constant.11.clone.1.scal_ref, bf16[2048,1024]{1,0:T(8,128)(2,1)} %refs_0_.11, f32[1,1024]{1,0:T(1,128)} %get-tuple-element.321.gain_ref.refs_1_, bf16[2048,2048]{1,0:T(8,128)(2,1)} %get-tuple-element.246.refs_1_.refs_2_, ...), custom_call_target="tpu_custom_call" | custom-call | flops 8589934592 | bytes 25165824 | tf_op jit(solution)/shard_map/norm_back1/pallas_call | solution.py:425
  413.8 18.8 %collective-permute-done.42 = bf16[4,256,512]{2,1,0:T(8,128)(2,1)S(1)} collective-permute-done((bf16[4,256,512]{2,1,0:T(8,128)(2,1)S(1)}, bf16[4,256,512]{2,1,0:T(8,128)(2,1)S(1)}, u32[]{:S(2)}, u32[]{:S(2)}) %collective-permute-start.42) | collective-permute-done | bytes 1048608 | tf_op jit(solution)/shard_map/ppermute | solution.py:411
  434.2 7.5 %norm_back0.1 = (f32[512,1024]{1,0:T(8,128)}, bf16[512,1024]{1,0:T(8,128)(2,1)}, f32[8,1024]{1,0:T(8,128)}) custom-call(s32[1]{0:T(128)} %constant.11.clone.1.scal_ref, bf16[512,1024]{1,0:T(8,128)(2,1)} %refs_0_.12, f32[1,1024]{1,0:T(1,128)} %get-tuple-element.319.gain_ref.refs_1_, bf16[512,1024]{1,0:T(8,128)(2,1)} %get-tuple-element.251.refs_1_.refs_2_, ...), custom_call_target="tpu_custom_call" | custom-call | flops 1073741824 | bytes 6291456 | tf_op jit(solution)/shard_map/norm_back0/pallas_call | solution.py:425
  442.7 10.3 %collective-permute-done.41 = bf16[4,256,512]{2,1,0:T(8,128)(2,1)} collective-permute-done((bf16[4,256,512]{2,1,0:T(8,128)(2,1)S(1)}, bf16[4,256,512]{2,1,0:T(8,128)(2,1)}, u32[]{:S(2)}, u32[]{:S(2)}) %collective-permute-start.41) | collective-permute-done | bytes 1048608 | tf_op jit(solution)/shard_map/ppermute | solution.py:411
  462.1 10.6 %collective-permute-done.48 = bf16[4,256,128]{2,1,0:T(8,128)(2,1)S(1)} collective-permute-done((bf16[4,256,128]{2,1,0:T(8,128)(2,1)S(1)}, bf16[4,256,128]{2,1,0:T(8,128)(2,1)S(1)}, u32[]{:S(2)}, u32[]{:S(2)}) %collective-permute-start.48) | collective-permute-done | bytes 262176 | tf_op jit(solution)/shard_map/ppermute | solution.py:411
  533.4 8.6 %collective-permute-done.68 = bf16[2,2,256,128]{3,2,1,0:T(8,128)(2,1)S(1)} collective-permute-done((bf16[2,2,256,128]{3,2,1,0:T(8,128)(2,1)S(1)}, bf16[2,2,256,128]{3,2,1,0:T(8,128)(2,1)S(1)}, u32[]{:S(2)}, u32[]{:S(2)}) %collective-permute-start.68) | collective-permute-done | bytes 262176 | tf_op jit(solution)/shard_map/ppermute | solution.py:411
  544.8 7.3 %collective-permute-done.67 = bf16[2,256,128]{2,1,0:T(8,128)(2,1)S(1)} collective-permute-done((bf16[2,256,128]{2,1,0:T(8,128)(2,1)S(1)}, bf16[2,256,128]{2,1,0:T(8,128)(2,1)S(1)}, u32[]{:S(2)}, u32[]{:S(2)}) %collective-permute-start.67) | collective-permute-done | bytes 131104 | tf_op jit(solution)/shard_map/ppermute | solution.py:411
  (352 shorter events, 299.2 us)
Async XLA Ops:
  4.9 34.9 %collective-permute-start.4 = (bf16[1024,256]{1,0:T(8,128)(2,1)}, bf16[1024,256]{1,0:T(8,128)(2,1)S(1)}, u32[]{:S(2)}, u32[]{:S(2)}) collective-permute-start(bf16[1024,256]{1,0:T(8,128)(2,1)} %get-tuple-element.161), channel_id=1, source_target_pairs={{0,1},{1,0},{2,3},{3,2},{4,5},{5,4},{6,7},{7,6},{8,9},{9,8},{10,11... | collective-permute-start | bytes 1572872 | tf_op jit(solution)/shard_map/ppermute | solution.py:411
  7.9 43.3 %collective-permute-start.8 = (bf16[256,1024]{1,0:T(8,128)(2,1)}, bf16[256,1024]{1,0:T(8,128)(2,1)S(1)}, u32[]{:S(2)}, u32[]{:S(2)}) collective-permute-start(bf16[256,1024]{1,0:T(8,128)(2,1)} %get-tuple-element.179), channel_id=1, source_target_pairs={{0,1},{1,0},{2,3},{3,2},{4,5},{5,4},{6,7},{7,6},{8,9},{9,8},{10,11... | collective-permute-start | bytes 1572872 | tf_op jit(solution)/shard_map/ppermute | solution.py:411
  7.9 29.8 %collective-permute-start = (bf16[1024,128]{1,0:T(8,128)(2,1)}, bf16[1024,128]{1,0:T(8,128)(2,1)S(1)}, u32[]{:S(2)}, u32[]{:S(2)}) collective-permute-start(bf16[1024,128]{1,0:T(8,128)(2,1)} %get-tuple-element.167), channel_id=1, source_target_pairs={{0,1},{1,0},{2,3},{3,2},{4,5},{5,4},{6,7},{7,6},{8,9},{9,8},{10,11... | collective-permute-start | bytes 786440 | tf_op jit(solution)/shard_map/ppermute | solution.py:411
  9.9 69.4 %collective-permute-start.12 = (bf16[1024,384]{1,0:T(8,128)(2,1)}, bf16[1024,384]{1,0:T(8,128)(2,1)S(1)}, u32[]{:S(2)}, u32[]{:S(2)}) collective-permute-start(bf16[1024,384]{1,0:T(8,128)(2,1)} %get-tuple-element.184), channel_id=1, source_target_pairs={{0,1},{1,0},{2,3},{3,2},{4,5},{5,4},{6,7},{7,6},{8,9},{9,8},{10,11... | collective-permute-start | bytes 2359304 | tf_op jit(solution)/shard_map/ppermute | solution.py:411
  99.7 27.1 %collective-permute-start.17 = (bf16[512,1024]{1,0:T(8,128)(2,1)S(1)}, bf16[512,1024]{1,0:T(8,128)(2,1)S(1)}, u32[]{:S(2)}, u32[]{:S(2)}) collective-permute-start(bf16[512,1024]{1,0:T(8,128)(2,1)S(1)} %copy-done.4), channel_id=1, source_target_pairs={{0,1},{1,0},{2,3},{3,2},{4,5},{5,4},{6,7},{7,6},{8,9},{9,8},{10,11... | collective-permute-start | bytes 3145736 | tf_op jit(solution)/shard_map/ppermute | solution.py:411
  124.7 25.5 %collective-permute-start.16 = (bf16[512,1024]{1,0:T(8,128)(2,1)}, bf16[512,1024]{1,0:T(8,128)(2,1)}, u32[]{:S(2)}, u32[]{:S(2)}) collective-permute-start(bf16[512,1024]{1,0:T(8,128)(2,1)} %get-tuple-element.199.x_ref.refs_0_), channel_id=1, source_target_pairs={{0,1},{1,0},{2,3},{3,2},{4,5},{5,4},{6,7},{7,6},{8,9},{9,8},{10,11... | collective-permute-start | bytes 3145736 | tf_op jit(solution)/shard_map/ppermute | solution.py:411
  126.2 40.4 %collective-permute-start.18 = (bf16[512,1024]{1,0:T(8,128)(2,1)S(1)}, bf16[512,1024]{1,0:T(8,128)(2,1)}, u32[]{:S(2)}, u32[]{:S(2)}) collective-permute-start(bf16[512,1024]{1,0:T(8,128)(2,1)S(1)} %copy-done.4), channel_id=1, source_target_pairs={{0,2},{1,3},{2,0},{3,1},{4,6},{5,7},{6,4},{7,5},{8,10},{9,11},{10,... | collective-permute-start | bytes 3145736 | tf_op jit(solution)/shard_map/ppermute | solution.py:411
  142.8 29.2 %collective-permute-start.20 = (bf16[512,2048]{1,0:T(8,128)(2,1)}, bf16[512,2048]{1,0:T(8,128)(2,1)S(1)}, u32[]{:S(2)}, u32[]{:S(2)}) collective-permute-start(bf16[512,2048]{1,0:T(8,128)(2,1)} %get-tuple-element.197.refs_4_), channel_id=1, source_target_pairs={{0,2},{1,3},{2,0},{3,1},{4,6},{5,7},{6,4},{7,5},{8,10},{9,11},{10,... | collective-permute-start | bytes 6291464 | tf_op jit(solution)/shard_map/ppermute | solution.py:411
  174.8 25.6 %collective-permute-start.26 = (bf16[512,1024]{1,0:T(8,128)(2,1)}, bf16[512,1024]{1,0:T(8,128)(2,1)S(1)}, u32[]{:S(2)}, u32[]{:S(2)}) collective-permute-start(bf16[512,1024]{1,0:T(8,128)(2,1)} %get-tuple-element.205), channel_id=1, source_target_pairs={{0,1},{1,0},{2,3},{3,2},{4,5},{5,4},{6,7},{7,6},{8,9},{9,8},{10,11... | collective-permute-start | bytes 3145736 | tf_op jit(solution)/shard_map/ppermute | solution.py:411
  229.6 26.4 %collective-permute-start.28 = (bf16[4,256,512]{2,1,0:T(8,128)(2,1)}, bf16[4,256,512]{2,1,0:T(8,128)(2,1)}, u32[]{:S(2)}, u32[]{:S(2)}) collective-permute-start(bf16[4,256,512]{2,1,0:T(8,128)(2,1)} %slice_bitcast_fusion.2), channel_id=1, source_target_pairs={{0,4},{1,5},{2,6},{3,7},{4,0},{5,1},{6,2},{7,3},{8,12},{9,13},{10,... | collective-permute-start | bytes 3145736 | tf_op jit(solution)/shard_map/ppermute | solution.py:411
  231.2 46.7 %collective-permute-start.30 = (bf16[4,256,512]{2,1,0:T(8,128)(2,1)}, bf16[4,256,512]{2,1,0:T(8,128)(2,1)S(1)}, u32[]{:S(2)}, u32[]{:S(2)}) collective-permute-start(bf16[4,256,512]{2,1,0:T(8,128)(2,1)} %slice_bitcast_fusion.1), channel_id=1, source_target_pairs={{0,4},{1,5},{2,6},{3,7},{4,0},{5,1},{6,2},{7,3},{8,12},{9,13},{10,... | collective-permute-start | bytes 3145736 | tf_op jit(solution)/shard_map/ppermute | solution.py:411
  327.3 30.0 %collective-permute-start.38 = (bf16[2,2,4,2,256,128]{5,4,3,2,1,0:T(8,128)(2,1)}, bf16[2,2,4,2,256,128]{5,4,3,2,1,0:T(8,128)(2,1)}, u32[]{:S(2)}, u32[]{:S(2)}) collective-permute-start(bf16[2,2,4,2,256,128]{5,4,3,2,1,0:T(8,128)(2,1)} %get-tuple-element.242), channel_id=1, source_target_pairs={{0,2},{1,3},{2,0},{3,1},{4,6},{5,7},{6,4},{7,5},{8,10},{9,11},{10,... | collective-permute-start | bytes 6291464 | tf_op jit(solution)/shard_map/ppermute | solution.py:411
  327.3 48.7 %collective-permute-start.39 = (bf16[2,4,4,256,128]{4,3,2,1,0:T(8,128)(2,1)S(1)}, bf16[2,4,4,256,128]{4,3,2,1,0:T(8,128)(2,1)}, u32[]{:S(2)}, u32[]{:S(2)}) collective-permute-start(bf16[2,4,4,256,128]{4,3,2,1,0:T(8,128)(2,1)S(1)} %fusion), channel_id=1, source_target_pairs={{0,1},{1,0},{2,3},{3,2},{4,5},{5,4},{6,7},{7,6},{8,9},{9,8},{10,11... | collective-permute-start | bytes 6291464 | tf_op jit(solution)/shard_map/ppermute | solution.py:411
  332.4 125.4 %collective-permute-start.46 = (bf16[512,1024]{1,0:T(8,128)(2,1)}, bf16[512,1024]{1,0:T(8,128)(2,1)}, u32[]{:S(2)}, u32[]{:S(2)}) collective-permute-start(bf16[512,1024]{1,0:T(8,128)(2,1)} %get-tuple-element.195), channel_id=1, source_target_pairs={{0,1},{1,0},{2,3},{3,2},{4,5},{5,4},{6,7},{7,6},{8,9},{9,8},{10,11... | collective-permute-start | bytes 3145736 | tf_op jit(solution)/shard_map/ppermute | solution.py:411
  351.7 27.5 %collective-permute-start.37 = (bf16[2,256,512]{2,1,0:T(8,128)(2,1)S(1)}, bf16[2,256,512]{2,1,0:T(8,128)(2,1)S(1)}, u32[]{:S(2)}, u32[]{:S(2)}) collective-permute-start(bf16[2,256,512]{2,1,0:T(8,128)(2,1)S(1)} %pad_maximum_fusion.3), channel_id=1, source_target_pairs={{0,8},{1,9},{2,10},{3,11},{4,12},{5,13},{6,14},{7,15},{8,0},{9,1},... | collective-permute-start | bytes 1572872 | tf_op jit(solution)/shard_map/ppermute | solution.py:411
  383.9 26.3 %collective-permute-start.43 = (bf16[4,4,256,128]{3,2,1,0:T(8,128)(2,1)}, bf16[4,4,256,128]{3,2,1,0:T(8,128)(2,1)}, u32[]{:S(2)}, u32[]{:S(2)}) collective-permute-start(bf16[4,4,256,128]{3,2,1,0:T(8,128)(2,1)} %fusion.1), channel_id=1, source_target_pairs={{0,4},{1,5},{2,6},{3,7},{4,0},{5,1},{6,2},{7,3},{8,12},{9,13},{10,... | collective-permute-start | bytes 3145736 | tf_op jit(solution)/shard_map/ppermute | solution.py:411
  384.4 48.2 %collective-permute-start.42 = (bf16[4,256,512]{2,1,0:T(8,128)(2,1)S(1)}, bf16[4,256,512]{2,1,0:T(8,128)(2,1)S(1)}, u32[]{:S(2)}, u32[]{:S(2)}) collective-permute-start(bf16[4,256,512]{2,1,0:T(8,128)(2,1)S(1)} %pad_maximum_fusion), channel_id=1, source_target_pairs={{0,4},{1,5},{2,6},{3,7},{4,0},{5,1},{6,2},{7,3},{8,12},{9,13},{10,... | collective-permute-start | bytes 3145736 | tf_op jit(solution)/shard_map/ppermute | solution.py:411
  406.6 46.4 %collective-permute-start.41 = (bf16[4,256,512]{2,1,0:T(8,128)(2,1)S(1)}, bf16[4,256,512]{2,1,0:T(8,128)(2,1)}, u32[]{:S(2)}, u32[]{:S(2)}) collective-permute-start(bf16[4,256,512]{2,1,0:T(8,128)(2,1)S(1)} %pad_maximum_fusion.1), channel_id=1, source_target_pairs={{0,4},{1,5},{2,6},{3,7},{4,0},{5,1},{6,2},{7,3},{8,12},{9,13},{10,... | collective-permute-start | bytes 3145736 | tf_op jit(solution)/shard_map/ppermute | solution.py:411
  408.1 47.9 %collective-permute-start.45 = (bf16[2,4,2,256,128]{4,3,2,1,0:T(8,128)(2,1)}, bf16[2,4,2,256,128]{4,3,2,1,0:T(8,128)(2,1)}, u32[]{:S(2)}, u32[]{:S(2)}) collective-permute-start(bf16[2,4,2,256,128]{4,3,2,1,0:T(8,128)(2,1)} %fusion.2), channel_id=1, source_target_pairs={{0,1},{1,0},{2,3},{3,2},{4,5},{5,4},{6,7},{7,6},{8,9},{9,8},{10,11... | collective-permute-start | bytes 3145736 | tf_op jit(solution)/shard_map/ppermute | solution.py:411
  412.9 40.2 %collective-permute-start.44 = (bf16[2,4,256,128]{3,2,1,0:T(8,128)(2,1)}, bf16[2,4,256,128]{3,2,1,0:T(8,128)(2,1)}, u32[]{:S(2)}, u32[]{:S(2)}) collective-permute-start(bf16[2,4,256,128]{3,2,1,0:T(8,128)(2,1)} %fusion.7), channel_id=1, source_target_pairs={{0,8},{1,9},{2,10},{3,11},{4,12},{5,13},{6,14},{7,15},{8,0},{9,1},... | collective-permute-start | bytes 1572872 | tf_op jit(solution)/shard_map/ppermute | solution.py:411
  432.7 43.4 %collective-permute-start.50 = (bf16[2,4,2,256,128]{4,3,2,1,0:T(8,128)(2,1)}, bf16[2,4,2,256,128]{4,3,2,1,0:T(8,128)(2,1)}, u32[]{:S(2)}, u32[]{:S(2)}) collective-permute-start(bf16[2,4,2,256,128]{4,3,2,1,0:T(8,128)(2,1)} %fusion.3), channel_id=1, source_target_pairs={{0,1},{1,0},{2,3},{3,2},{4,5},{5,4},{6,7},{7,6},{8,9},{9,8},{10,11... | collective-permute-start | bytes 3145736 | tf_op jit(solution)/shard_map/ppermute | solution.py:411
  472.8 25.6 %collective-permute-start.59 = (bf16[4,256,512]{2,1,0:T(8,128)(2,1)S(1)}, bf16[4,256,512]{2,1,0:T(8,128)(2,1)}, u32[]{:S(2)}, u32[]{:S(2)}) collective-permute-start(bf16[4,256,512]{2,1,0:T(8,128)(2,1)S(1)} %pad_maximum_fusion.1), channel_id=1, source_target_pairs={{0,2},{1,3},{2,0},{3,1},{4,6},{5,7},{6,4},{7,5},{8,10},{9,11},{10,... | collective-permute-start | bytes 3145736 | tf_op jit(solution)/shard_map/ppermute | solution.py:411
  506.4 26.8 %collective-permute-start.69 = (bf16[4,4,256,128]{3,2,1,0:T(8,128)(2,1)S(1)}, bf16[4,4,256,128]{3,2,1,0:T(8,128)(2,1)S(1)}, u32[]{:S(2)}, u32[]{:S(2)}) collective-permute-start(bf16[4,4,256,128]{3,2,1,0:T(8,128)(2,1)S(1)} %pad_maximum_fusion.2.refs_0_), channel_id=1, source_target_pairs={{0,4},{1,5},{2,6},{3,7},{4,0},{5,1},{6,2},{7,3},{8,12},{9,13},{10,... | collective-permute-start | bytes 3145736 | tf_op jit(solution)/shard_map/ppermute | solution.py:411
  520.4 31.9 %collective-permute-start.72 = (bf16[4,4,256,128]{3,2,1,0:T(8,128)(2,1)S(1)}, bf16[4,4,256,128]{3,2,1,0:T(8,128)(2,1)S(1)}, u32[]{:S(2)}, u32[]{:S(2)}) collective-permute-start(bf16[4,4,256,128]{3,2,1,0:T(8,128)(2,1)S(1)} %pad_maximum_fusion.2.refs_0_), channel_id=1, source_target_pairs={{0,2},{1,3},{2,0},{3,1},{4,6},{5,7},{6,4},{7,5},{8,10},{9,11},{10,... | collective-permute-start | bytes 3145736 | tf_op jit(solution)/shard_map/ppermute | solution.py:411
  (115 other events, 1345.8 us)
